TPU v7x, 128 devices: a whole 4x4x4 slice. The times are simulated.
128 devices in a mesh: fsdp: 32 (over z, y, x_lo), sp: 4 (over x_hi, core).
Axes of the slice: x: 4 (x_hi: 2, x_lo: 2; x = x_hi * 2 + x_lo), y: 4, z: 4, core: 2. Of those that a mesh axis runs over, the one named last changes fastest.
Arguments:
- tokens: bfloat16 [32768, 768], P(('fsdp', 'sp')), may hold values from -60 to 60
- lengths: int32 [32], P('fsdp'), may hold values from 512 to 1024, as said below
- w_qkv: bfloat16 [768, 2304], P('fsdp'), may hold values from -0.21875 to 0.21875
- w_out: bfloat16 [768, 768], P('fsdp'), may hold values from -1.25 to 1.25
- w_in: bfloat16 [768, 3072], P('fsdp'), may hold values from -0.21875 to 0.21875
- w_back: bfloat16 [3072, 768], P('fsdp'), may hold values from -0.109375 to 0.109375
- bias_q: bfloat16 [768], P('fsdp'), may hold values from -3 to 3
- bias_v: bfloat16 [768], P('fsdp'), may hold values from -0.59765625 to 0.59765625
- bias_o: bfloat16 [768], P('fsdp'), may hold values from -3 to 3
- gain_one: bfloat16 [768], P('fsdp'), may hold values from 0.5 to 1.5
- shift_one: bfloat16 [768], P('fsdp'), may hold values from -3 to 3
- bias_in: bfloat16 [3072], P('fsdp'), may hold values from -3 to 3
- bias_back: bfloat16 [768], P('fsdp'), may hold values from -3 to 3
- gain_two: bfloat16 [768], P('fsdp'), may hold values from 0.5 to 1.5
- shift_two: bfloat16 [768], P('fsdp'), may hold values from -3 to 3
- cotangent: bfloat16 [32768, 768], P(('fsdp', 'sp')), may hold values from -24 to 24
Outputs:
- output: bfloat16 [32768, 768], P(('fsdp', 'sp'))
- grad_tokens: bfloat16 [32768, 768], P(('fsdp', 'sp'))
- grad_qkv: float32 [768, 2304], P('fsdp')
- grad_out: float32 [768, 768], P('fsdp')
- grad_in: float32 [768, 3072], P('fsdp')
- grad_back: float32 [3072, 768], P('fsdp')
- grad_bias_q: float32 [768], P('fsdp')
- grad_bias_v: float32 [768], P('fsdp')
- grad_bias_o: float32 [768], P('fsdp')
- grad_gain_one: float32 [768], P('fsdp')
- grad_shift_one: float32 [768], P('fsdp')
- grad_bias_in: float32 [3072], P('fsdp')
- grad_bias_back: float32 [768], P('fsdp')
- grad_gain_two: float32 [768], P('fsdp')
- grad_shift_two: float32 [768], P('fsdp')
Inputs may be any that keep to these rules, and one draw needn't show every extreme that they name: `lengths`: each sequence's valid tokens are its first ones.
All inputs are finite; a program needn't handle non-finite values.
Results may differ from a plain program's by a relative error of at most 0.025.
The roundings to bfloat16 on the way count: a program that leaves them out, or rounds other values in their place, can miss the bound.
Values may be sent and summed in bfloat16 or wider, within the bound.
No kernel may reach another device: no remote copies, remote signals or barrier semaphores. Data moves between devices by JAX's collectives and lax.ppermute only.
A program may use at most 128 MiB of HBM per device.

v0:
```python
import jax
import jax.numpy as jnp
from jax import lax
from jax.sharding import Mesh
from jax.sharding import PartitionSpec as P

H = 12
HD = 64
SP = ("sp_0", "sp_1")
FSDP_SP = ("fsdp", "sp_0", "sp_1")


EPS = 1e-05


def in_one_piece(arrays, axis, dim, along):
    widths = [a.shape[along] for a in arrays]
    both = jnp.concatenate(arrays, axis=along)
    filled = lax.all_gather(both, axis, axis=dim, tiled=True)
    return tuple(jnp.split(filled, [sum(widths[:k]) for k in range(1, len(widths))], axis=along))


def cut_along(value, dim, count):
    lengths = value.shape
    blocks = value.reshape(*lengths[:dim], count, lengths[dim] // count, *lengths[dim + 1 :])
    return jnp.moveaxis(blocks, dim, 0)


def laid_out(blocks, dim):
    lengths = list(blocks.shape[1:])
    lengths[dim] *= blocks.shape[0]
    return jnp.moveaxis(blocks, 0, dim).reshape(lengths)


def turned_blocks(blocks, axes, sequence):
    lengths = [lax.axis_size(a) for a in axes]
    blocks = blocks.reshape(*lengths, *blocks.shape[1:])
    for k in sequence:
        blocks = lax.all_to_all(blocks, axes[k], split_axis=k, concat_axis=k, tiled=True)
    return blocks.reshape(-1, *blocks.shape[len(axes) :])


def exchange_by_chip(value, groups, sequence, split_dim, concat_dim):
    count = lax.axis_size(groups[0]) * lax.axis_size(groups[1])
    blocks = cut_along(value, split_dim, count)
    return laid_out(turned_blocks(blocks, groups, sequence), concat_dim)


def sent_together(arrays, axis, dim, along):
    both = jnp.concatenate(arrays, axis=along)
    filled, at, gathered = (lax.psum_scatter(both, axis, scatter_dimension=dim, tiled=True), 0, [])
    for a in arrays:
        gathered.append(lax.slice_in_dim(filled, at, at + a.shape[along], axis=along))
        at += a.shape[along]
    return tuple(gathered)


def sent_to_all(value, axis):
    copies = jnp.broadcast_to(value, (lax.axis_size(axis), *value.shape))
    return lax.all_to_all(copies, axis, split_axis=0, concat_axis=0, tiled=True)


def taken_together(value, axis):
    return sent_to_all(value, axis).astype(jnp.float32).sum(axis=0)


def layer_norm(hidden, gain, shift):
    mean = jnp.mean(hidden, axis=-1, keepdims=True)
    centred = hidden - mean
    variance = jnp.mean(centred * centred, axis=-1, keepdims=True)
    inverse = lax.rsqrt(variance + EPS)
    normed = centred * inverse
    return (normed * gain + shift, normed, inverse)


def norm_back(grad, normed, inverse, gain):
    scaled = grad * gain
    first = jnp.mean(scaled, axis=-1, keepdims=True)
    second = jnp.mean(scaled * normed, axis=-1, keepdims=True)
    return inverse * (scaled - first - normed * second)


def gelu_exact(value):
    return jax.nn.gelu(value, approximate=False)


def contract_rows(left, right):
    return lax.dot_general(
        left, right, (((0,), (0,)), ((), ())), preferred_element_type=jnp.float32
    )


def contract_cols(left, right):
    return lax.dot_general(
        left, right, (((1,), (1,)), ((), ())), preferred_element_type=jnp.float32
    )


def attend_heads(query, keys, values, valid, scale):
    total = query.shape[0]
    block = min(512, total)
    count = total // block

    def one(index):
        rows = lax.dynamic_slice_in_dim(query, index * block, block, 0)
        scores = jnp.einsum("qhd,khd->hqk", rows, keys, preferred_element_type=jnp.float32) * scale
        scores = jnp.where(valid[None, None, :], scores, -jnp.inf)
        top = jnp.max(scores, axis=-1, keepdims=True)
        expo = jnp.exp(scores - top)
        summed = jnp.sum(expo, axis=-1, keepdims=True)
        probs = (expo / summed).astype(jnp.bfloat16)
        context = jnp.einsum(
            "hqk,khd->qhd", probs, values, preferred_element_type=jnp.float32
        ).astype(jnp.bfloat16)
        return (context, (top + jnp.log(summed))[..., 0])

    context, logsum = lax.map(one, jnp.arange(count, dtype=jnp.int32))
    return (context.reshape(query.shape), logsum)


def attend_back(query, keys, values, context, logsum, grad_context, valid, scale):
    total = query.shape[0]
    block = min(512, total)
    count = total // block

    def one(carry, index):
        grad_keys, grad_values = carry
        rows = lax.dynamic_slice_in_dim(query, index * block, block, 0)
        outs = lax.dynamic_slice_in_dim(context, index * block, block, 0)
        grads = lax.dynamic_slice_in_dim(grad_context, index * block, block, 0)
        logs = logsum[index]
        scores = jnp.einsum("qhd,khd->hqk", rows, keys, preferred_element_type=jnp.float32) * scale
        scores = jnp.where(valid[None, None, :], scores, -jnp.inf)
        probs = jnp.exp(scores - logs[..., None])
        probs_b = probs.astype(jnp.bfloat16)
        grad_values = grad_values + jnp.einsum(
            "hqk,qhd->khd", probs_b, grads, preferred_element_type=jnp.float32
        )
        grad_probs = jnp.einsum("qhd,khd->hqk", grads, values, preferred_element_type=jnp.float32)
        delta = jnp.sum(grads.astype(jnp.float32) * outs.astype(jnp.float32), axis=-1).T
        grad_scores = (probs * (grad_probs - delta[..., None])).astype(jnp.bfloat16)
        grad_rows = (
            jnp.einsum("hqk,khd->qhd", grad_scores, keys, preferred_element_type=jnp.float32)
            * scale
        ).astype(jnp.bfloat16)
        grad_keys = (
            grad_keys
            + jnp.einsum("hqk,qhd->khd", grad_scores, rows, preferred_element_type=jnp.float32)
            * scale
        )
        return ((grad_keys, grad_values), grad_rows)

    zero = jnp.zeros(query.shape, jnp.float32)
    (grad_keys, grad_values), grad_query = lax.scan(
        one, (zero, zero), jnp.arange(count, dtype=jnp.int32)
    )
    return (
        grad_query.reshape(query.shape),
        grad_keys.astype(jnp.bfloat16),
        grad_values.astype(jnp.bfloat16),
    )


def body(
    tokens,
    lengths,
    w_qkv,
    w_out,
    w_in,
    w_back,
    bias_q,
    bias_v,
    bias_o,
    gain_one,
    shift_one,
    bias_in,
    bias_back,
    gain_two,
    shift_two,
    cotangent,
):
    f32 = jnp.float32
    whole = (
        *in_one_piece((w_qkv, w_out, w_in), "fsdp", 0, 1),
        lax.all_gather(w_back, "fsdp", axis=0, tiled=True),
        lax.all_gather(bias_q, "fsdp", axis=0, tiled=True),
        lax.all_gather(bias_v, "fsdp", axis=0, tiled=True),
        lax.all_gather(bias_o, "fsdp", axis=0, tiled=True),
        lax.all_gather(gain_one, "fsdp", axis=0, tiled=True),
        lax.all_gather(shift_one, "fsdp", axis=0, tiled=True),
        lax.all_gather(bias_in, "fsdp", axis=0, tiled=True),
        lax.all_gather(bias_back, "fsdp", axis=0, tiled=True),
        lax.all_gather(gain_two, "fsdp", axis=0, tiled=True),
        lax.all_gather(shift_two, "fsdp", axis=0, tiled=True),
    )
    rows, width = tokens.shape
    groups = lax.axis_size(SP)
    local = H // groups
    span = local * HD
    total = rows * groups
    scale = HD ** (-0.5)
    w_qkv_all, w_out_all, w_in_all, w_back_all = (whole[0], whole[1], whole[2], whole[3])
    b_q, b_v, b_o, g_one, s_one, b_in, b_back, g_two, s_two = [
        piece.astype(f32) for piece in whole[4:]
    ]
    bias_qkv = jnp.concatenate([b_q, jnp.zeros((width,), f32), b_v])
    packed = (jnp.dot(tokens, w_qkv_all, preferred_element_type=f32) + bias_qkv).astype(
        jnp.bfloat16
    )
    headed = exchange_by_chip(packed.reshape(rows, 3, groups, span), ("sp_0", "sp_1"), (1, 0), 2, 0)
    headed = headed.reshape(total, 3, local, HD)
    query = headed[:, 0]
    keys = headed[:, 1]
    values = headed[:, 2]
    valid = jnp.arange(total, dtype=jnp.int32) < lengths[0]
    context, logsum = attend_heads(query, keys, values, valid, scale)
    back_rows = lax.all_to_all(
        context.reshape(total, 1, span), SP, split_axis=0, concat_axis=1, tiled=True
    )
    ctx_rows = back_rows.reshape(rows, width)
    h_one = tokens.astype(f32) + jnp.dot(ctx_rows, w_out_all, preferred_element_type=f32) + b_o
    y_one, n_one, i_one = layer_norm(h_one, g_one, s_one)
    y_oneb = y_one.astype(jnp.bfloat16)
    pre = jnp.dot(y_oneb, w_in_all, preferred_element_type=f32) + b_in
    act = gelu_exact(pre).astype(jnp.bfloat16)
    h_two = y_oneb.astype(f32) + jnp.dot(act, w_back_all, preferred_element_type=f32) + b_back
    out, n_two, i_two = layer_norm(h_two, g_two, s_two)
    again = (
        *in_one_piece((w_qkv, w_out, w_in), "fsdp", 0, 1),
        lax.all_gather(w_back, "fsdp", axis=0, tiled=True),
        lax.all_gather(bias_q, "fsdp", axis=0, tiled=True),
        lax.all_gather(bias_v, "fsdp", axis=0, tiled=True),
        lax.all_gather(bias_o, "fsdp", axis=0, tiled=True),
        lax.all_gather(gain_one, "fsdp", axis=0, tiled=True),
        lax.all_gather(shift_one, "fsdp", axis=0, tiled=True),
        lax.all_gather(bias_in, "fsdp", axis=0, tiled=True),
        lax.all_gather(bias_back, "fsdp", axis=0, tiled=True),
        lax.all_gather(gain_two, "fsdp", axis=0, tiled=True),
        lax.all_gather(shift_two, "fsdp", axis=0, tiled=True),
    )
    w_qkv_b, w_out_b, w_in_b, w_back_b = (again[0], again[1], again[2], again[3])
    g_one_b = again[7].astype(f32)
    g_two_b = again[11].astype(f32)
    grad = cotangent.astype(f32)
    d_g2 = jnp.sum(grad * n_two, axis=0)
    d_s2 = jnp.sum(grad, axis=0)
    dh_two = norm_back(grad, n_two, i_two, g_two_b)
    d_bb = jnp.sum(dh_two, axis=0)
    dh_twob = dh_two.astype(jnp.bfloat16)
    d_wb = contract_rows(act, dh_twob)
    d_act = contract_cols(dh_twob, w_back_b)
    d_pre = jax.vjp(gelu_exact, pre)[1](d_act)[0]
    d_bi = jnp.sum(d_pre, axis=0)
    d_preb = d_pre.astype(jnp.bfloat16)
    d_wi = contract_rows(y_oneb, d_preb)
    dy_one = dh_two + contract_cols(d_preb, w_in_b)
    d_g1 = jnp.sum(dy_one * n_one, axis=0)
    d_s1 = jnp.sum(dy_one, axis=0)
    dh_one = norm_back(dy_one, n_one, i_one, g_one_b)
    d_bo = jnp.sum(dh_one, axis=0)
    dh_oneb = dh_one.astype(jnp.bfloat16)
    d_wo = contract_rows(ctx_rows, dh_oneb)
    d_ctx = contract_cols(dh_oneb, w_out_b).astype(jnp.bfloat16)
    grad_heads = lax.all_to_all(
        d_ctx.reshape(rows, groups, span), SP, split_axis=1, concat_axis=0, tiled=True
    )
    grad_heads = grad_heads.reshape(total, local, HD)
    g_query, g_keys, g_values = attend_back(
        query, keys, values, context, logsum, grad_heads, valid, scale
    )
    stacked = jnp.stack([g_query, g_keys, g_values], axis=1).reshape(total, 3, 1, span)
    d_packed = lax.all_to_all(stacked, SP, split_axis=0, concat_axis=2, tiled=True).reshape(
        rows, 3 * width
    )
    d_bq = jnp.sum(d_packed[:, :width].astype(f32), axis=0)
    d_bv = jnp.sum(d_packed[:, 2 * width :].astype(f32), axis=0)
    d_wq = contract_rows(tokens, d_packed)
    d_x = (dh_one + contract_cols(d_packed, w_qkv_b)).astype(jnp.bfloat16)
    shares = (
        *tuple(
            (
                part.astype(jnp.float32)
                for part in sent_together(
                    (
                        d_wq.astype(jnp.bfloat16),
                        d_wo.astype(jnp.bfloat16),
                        d_wi.astype(jnp.bfloat16),
                    ),
                    "fsdp",
                    0,
                    1,
                )
            )
        ),
        lax.psum_scatter(d_wb.astype(jnp.bfloat16), "fsdp", scatter_dimension=0, tiled=True).astype(
            jnp.float32
        ),
        lax.psum_scatter(d_bq.astype(jnp.bfloat16), "fsdp", scatter_dimension=0, tiled=True).astype(
            jnp.float32
        ),
        lax.psum_scatter(d_bv.astype(jnp.bfloat16), "fsdp", scatter_dimension=0, tiled=True).astype(
            jnp.float32
        ),
        lax.psum_scatter(d_bo.astype(jnp.bfloat16), "fsdp", scatter_dimension=0, tiled=True).astype(
            jnp.float32
        ),
        lax.psum_scatter(d_g1.astype(jnp.bfloat16), "fsdp", scatter_dimension=0, tiled=True).astype(
            jnp.float32
        ),
        lax.psum_scatter(d_s1.astype(jnp.bfloat16), "fsdp", scatter_dimension=0, tiled=True).astype(
            jnp.float32
        ),
        lax.psum_scatter(d_bi.astype(jnp.bfloat16), "fsdp", scatter_dimension=0, tiled=True).astype(
            jnp.float32
        ),
        lax.psum_scatter(d_bb.astype(jnp.bfloat16), "fsdp", scatter_dimension=0, tiled=True).astype(
            jnp.float32
        ),
        lax.psum_scatter(d_g2.astype(jnp.bfloat16), "fsdp", scatter_dimension=0, tiled=True).astype(
            jnp.float32
        ),
        lax.psum_scatter(d_s2.astype(jnp.bfloat16), "fsdp", scatter_dimension=0, tiled=True).astype(
            jnp.float32
        ),
    )
    owned = (
        taken_together(shares[0].astype(jnp.bfloat16), SP).astype(jnp.float32),
        taken_together(shares[1].astype(jnp.bfloat16), SP).astype(jnp.float32),
        taken_together(shares[2].astype(jnp.bfloat16), SP).astype(jnp.float32),
        taken_together(shares[3].astype(jnp.bfloat16), SP).astype(jnp.float32),
        taken_together(shares[4].astype(jnp.bfloat16), SP).astype(jnp.float32),
        taken_together(shares[5].astype(jnp.bfloat16), SP).astype(jnp.float32),
        taken_together(shares[6].astype(jnp.bfloat16), SP).astype(jnp.float32),
        taken_together(shares[7].astype(jnp.bfloat16), SP).astype(jnp.float32),
        taken_together(shares[8].astype(jnp.bfloat16), SP).astype(jnp.float32),
        taken_together(shares[9].astype(jnp.bfloat16), SP).astype(jnp.float32),
        taken_together(shares[10].astype(jnp.bfloat16), SP).astype(jnp.float32),
        taken_together(shares[11].astype(jnp.bfloat16), SP).astype(jnp.float32),
        taken_together(shares[12].astype(jnp.bfloat16), SP).astype(jnp.float32),
    )
    return (
        out.astype(jnp.bfloat16),
        d_x,
        owned[0],
        owned[1],
        owned[2],
        owned[3],
        owned[4],
        owned[5],
        owned[6],
        owned[7],
        owned[8],
        owned[9],
        owned[10],
        owned[11],
        owned[12],
    )


def solution(mesh):
    split = Mesh(mesh.devices.reshape(mesh.shape["fsdp"], 2, 2), ("fsdp", "sp_0", "sp_1"))
    in_specs = (
        P(FSDP_SP, None),
        P("fsdp"),
        P("fsdp", None),
        P("fsdp", None),
        P("fsdp", None),
        P("fsdp", None),
        P("fsdp"),
        P("fsdp"),
        P("fsdp"),
        P("fsdp"),
        P("fsdp"),
        P("fsdp"),
        P("fsdp"),
        P("fsdp"),
        P("fsdp"),
        P(FSDP_SP, None),
    )
    out_specs = (
        P(FSDP_SP, None),
        P(FSDP_SP, None),
        P("fsdp", None),
        P("fsdp", None),
        P("fsdp", None),
        P("fsdp", None),
        P("fsdp"),
        P("fsdp"),
        P("fsdp"),
        P("fsdp"),
        P("fsdp"),
        P("fsdp"),
        P("fsdp"),
        P("fsdp"),
        P("fsdp"),
    )
    return jax.shard_map(body, mesh=split, in_specs=in_specs, out_specs=out_specs, check_vma=False)
```

profile of v0, /device:TPU:1, one launch (start us, length us, event | category | flops | bytes accessed | tf_op | source)
XLA Modules:
  0.0 867.1 jit_solution(297504318716623446)
XLA Ops:
  19.1 144.9 %all-reduce.19 = (bf16[768]{0:T(1024)(128)(2,1)S(1)}, bf16[768]{0:T(1024)(128)(2,1)S(1)}, bf16[768]{0:T(1024)(128)(2,1)}, bf16[768]{0:T(1024)(128)(2,1)}, bf16[7...) all-reduce(bf16[768]{0:T(1024)(128)(2,1)S(1)} %dynamic-update-slice, ...), channel_id=1, replica_groups=mesh['fsdp'=32,'sp_0'=2,'sp_1'=2] {'fsdp'}, use_global_device_ids=true, to_apply=%add.1 | all-reduce | flops 8448 | bytes 33792
  164.0 66.4 %all-gather.3.cloned.1.call-done = bf16[768,6144]{1,0:T(8,128)(2,1)} async-done(((bf16[24,6144]{1,0:T(8,128)(2,1)}), bf16[768,6144]{1,0:T(8,128)(2,1)}) %all-gather.3.cloned.1.call-update) | async-done | bytes 9437200 | tf_op jit(solution)/shard_map/all_gather | solution.py:19
  235.1 5.5 all_to_all.129
  246.7 29.1 %all-to-all-done.1 = bf16[2,2,256,3,1,192]{2,1,5,3,4,0:T(2,128)(2,1)S(1)} async-done(((bf16[2,2,256,3,1,192]{2,1,5,3,4,0:T(2,128)(2,1)}), bf16[2,2,256,3,1,192]{2,1,5,3,4,0:T(2,128)(2,1)S(1)}, u32[]{:S(2)}, u32[]{:S(2)}) %all-to-all-start.1) | async-done | bytes 1179680 | tf_op jit(solution)/shard_map/all_to_all | solution.py:39
  277.6 13.2 %while.28 = (s32[]{:T(128)}, bf16[2,512,3,64]{1,3,2,0:T(8,128)(2,1)S(1)}, f32[2,3,512]{2,1,0:T(4,128)S(1)}, s32[2]{0:T(128)S(1)}, bf16[1024,3,64]{0,2,1:T(8,128)...) while((s32[]{:T(128)}, ...), condition=%wide.region_3.4_spmd.clone, body=%wide.region_0.3_spmd.clone.sunk | while | flops 421625344 | bytes 20117704 | solution.py:117
  295.2 5.1 all-to-all-start.2
  301.0 11.4 %all-to-all-done.2 = bf16[4,2,24576]{2,1,0:T(2,128)(2,1)S(1)} async-done(((bf16[4,2,24576]{2,1,0:T(2,128)(2,1)}), bf16[4,2,24576]{2,1,0:T(2,128)(2,1)S(1)}, u32[]{:S(2)}, u32[]{:S(2)}) %all-to-all-start.2) | async-done | bytes 393248 | tf_op jit(solution)/shard_map/all_to_all | solution.py:217
  316.5 11.6 %multiply_convert_fusion.1 = (bf16[256,3072]{1,0:T(8,128)(2,1)S(1)}, f32[256,3072]{1,0:T(8,128)}, f32[256,3072]{1,0:T(8,128)}) fusion(f32[3072]{0:T(1024)S(1)} %copy-done.29, bf16[768,6144]{1,0:T(8,128)(2,1)} %all-gather.3.cloned.1.call-done, f32[256,768]{1,0:T(8,128)S(1)} %get-tuple-element.269, f32[768]{0:T(1024)S(1)} %convert_element_type.220, ...), kind=kOutput, calls=%fused_computation.61 | convolution fusion | flops 1260847104 | bytes 13389824 | tf_op jit(solution)/shard_map/dot_general | solution.py:224
  328.0 59.0 %all-gather.5.cloned.1.call-done = bf16[3072,768]{1,0:T(8,128)(2,1)} async-done(((bf16[96,768]{1,0:T(8,128)(2,1)}), bf16[3072,768]{1,0:T(8,128)(2,1)}) %all-gather.5.cloned.1.call-update) | async-done | bytes 4718608 | tf_op jit(solution)/shard_map/all_gather | solution.py:185
  398.6 6.9 fusion.95
  405.5 5.2 multiply_reduce_fusion.1
  414.5 21.6 %all-to-all-start.3 = ((bf16[256,4,192]{0,2,1:T(8,128)(2,1)}), bf16[256,4,192]{0,2,1:T(8,128)(2,1)}, u32[]{:S(2)}, u32[]{:S(2)}) async-start(bf16[256,4,192]{0,2,1:T(8,128)(2,1)} %bitcast.12), calls=%async_computation.3 | async-start | bytes 786432 | tf_op jit(solution)/shard_map/all_to_all | solution.py:264
  437.2 8.7 %all-to-all-done.3 = bf16[256,4,192]{0,2,1:T(8,128)(2,1)} async-done(((bf16[256,4,192]{0,2,1:T(8,128)(2,1)}), bf16[256,4,192]{0,2,1:T(8,128)(2,1)}, u32[]{:S(2)}, u32[]{:S(2)}) %all-to-all-start.3) | async-done | bytes 393248 | tf_op jit(solution)/shard_map/all_to_all | solution.py:264
  451.3 26.1 %while.29 = (s32[]{:T(128)}, f32[1024,3,64]{0,2,1:T(8,128)S(1)}, f32[1024,3,64]{0,2,1:T(8,128)}, bf16[2,512,3,64]{1,3,2,0:T(8,128)(2,1)}, s32[2]{0:T(128)}, /*in...) while((s32[]{:T(128)}, f32[1024,3,64]{0,2,1:T(8,128)S(1)}, ...), condition=%wide.region_14.15_spmd.clone, body=%wide.region_12.14_spmd.clone.sunk | while | flops 1023933952 | bytes 46642640 | solution.py:154
  483.1 6.5 all-to-all-start.4
  491.6 5.2 convolution_convert_fusion.1
  496.9 39.6 %all-to-all-done.4 = bf16[1024,3,1,192]{3,1,2,0:T(4,128)(2,1)} async-done(((bf16[1024,3,1,192]{3,1,2,0:T(4,128)(2,1)}), bf16[1024,3,1,192]{3,1,2,0:T(4,128)(2,1)}, u32[]{:S(2)}, u32[]{:S(2)}) %all-to-all-start.4) | async-done | bytes 1179680 | tf_op jit(solution)/shard_map/all_to_all | solution.py:272
  547.7 9.2 %pad_maximum_fusion = bf16[768,6144]{1,0:T(8,128)(2,1)} fusion(bf16[768,3072]{1,0:T(8,128)(2,1)} %convolution_convert_fusion.1, bf16[768,768]{1,0:T(8,128)(2,1)} %copy.160, bf16[768,2304]{1,0:T(8,128)(2,1)} %copy.159), kind=kLoop, calls=%fused_computation.46 | loop fusion | flops 28311552 | bytes 18874368 | tf_op jit(solution)/shard_map/concatenate | solution.py:50
  559.1 140.3 %all-reduce.18 = (bf16[768]{0:T(1024)(128)(2,1)S(1)}, bf16[768]{0:T(1024)(128)(2,1)S(1)}, bf16[768]{0:T(1024)(128)(2,1)S(1)}, bf16[768]{0:T(1024)(128)(2,1)S(1)}...) all-reduce(bf16[768]{0:T(1024)(128)(2,1)S(1)} %dynamic-update-slice, ...), channel_id=1, replica_groups=mesh['fsdp'=32,'sp_0'=2,'sp_1'=2] {'fsdp'}, use_global_device_ids=true, to_apply=%add.8 | all-reduce | flops 9984 | bytes 39936
  700.2 26.9 %all-to-all-start.9 = ((bf16[4,1,24]{2,1,0:T(2,128)(2,1)}), bf16[4,1,24]{2,1,0:T(2,128)(2,1)S(1)}, u32[]{:S(2)}, u32[]{:S(2)}) async-start(bf16[4,1,24]{2,1,0:T(2,128)(2,1)} %broadcast_in_dim.107), calls=%async_computation.11 | async-start | bytes 4096 | tf_op jit(solution)/shard_map/all_to_all | solution.py:60
  772.6 4.8 all-to-all-done.15
  790.6 4.8 all-to-all-done.17
  837.9 6.0 all-to-all-done.5
  851.9 7.3 all-to-all-done.7
  (289 shorter events, 216.4 us)
Async XLA Ops:
  7.2 223.2 %all-gather.3.cloned.1.call-start = ((), (), s32[]{:S(2)}) async-start(), calls=%async_computation.20 | async-start | bytes 9732096 | tf_op jit(solution)/shard_map/all_gather | solution.py:19
  9.0 378.0 %all-gather.5.cloned.1.call-start = ((), (), s32[]{:S(2)}) async-start(), calls=%async_computation.21 | async-start | bytes 4866048 | tf_op jit(solution)/shard_map/all_gather | solution.py:185
  242.8 33.0 %all-to-all-start.1 = ((bf16[2,2,256,3,1,192]{2,1,5,3,4,0:T(2,128)(2,1)}), bf16[2,2,256,3,1,192]{2,1,5,3,4,0:T(2,128)(2,1)S(1)}, u32[]{:S(2)}, u32[]{:S(2)}) async-start(bf16[2,2,256,3,1,192]{2,1,5,3,4,0:T(2,128)(2,1)} %copy.146), calls=%async_computation.1 | async-start | bytes 2359296 | tf_op jit(solution)/shard_map/all_to_all | solution.py:39
  295.2 17.2 %all-to-all-start.2 = ((bf16[4,2,24576]{2,1,0:T(2,128)(2,1)}), bf16[4,2,24576]{2,1,0:T(2,128)(2,1)S(1)}, u32[]{:S(2)}, u32[]{:S(2)}) async-start(bf16[4,2,24576]{2,1,0:T(2,128)(2,1)} %reshape.240), calls=%async_computation.2 | async-start | bytes 786432 | tf_op jit(solution)/shard_map/all_to_all | solution.py:217
  300.3 504.1 %reduce-scatter.5.cloned.1.call-start = ((), (), s32[]{:S(2)}) async-start(), calls=%async_computation.23 | async-start | bytes 4866048 | tf_op jit(solution)/shard_map/reduce_scatter | solution.py:295
  316.2 94.5 %copy-start.23 = (f32[256]{0:T(256)}, f32[256]{0:T(256)S(1)}, u32[]{:S(2)}) copy-start(f32[256]{0:T(256)S(1)} %broadcast_multiply_fusion.5) | copy-start | bytes 3076
  316.5 94.2 %copy-start.27 = (f32[256]{0:T(256)}, f32[256]{0:T(256)S(1)}, u32[]{:S(2)}) copy-start(f32[256]{0:T(256)S(1)} %add_rsqrt_fusion.1) | copy-start | bytes 3076
  414.5 31.4 %all-to-all-start.3 = ((bf16[256,4,192]{0,2,1:T(8,128)(2,1)}), bf16[256,4,192]{0,2,1:T(8,128)(2,1)}, u32[]{:S(2)}, u32[]{:S(2)}) async-start(bf16[256,4,192]{0,2,1:T(8,128)(2,1)} %bitcast.12), calls=%async_computation.3 | async-start | bytes 786432 | tf_op jit(solution)/shard_map/all_to_all | solution.py:264
  483.1 53.4 %all-to-all-start.4 = ((bf16[1024,3,1,192]{3,1,2,0:T(4,128)(2,1)}), bf16[1024,3,1,192]{3,1,2,0:T(4,128)(2,1)}, u32[]{:S(2)}, u32[]{:S(2)}) async-start(bf16[1024,3,1,192]{3,1,2,0:T(4,128)(2,1)} %copy.156), calls=%async_computation.4 | async-start | bytes 4194304 | tf_op jit(solution)/shard_map/all_to_all | solution.py:272
  489.6 327.0 %reduce-scatter.3.cloned.1.call-start = ((), (), s32[]{:S(2)}) async-start(), calls=%async_computation.22 | async-start | bytes 9732096 | tf_op jit(solution)/shard_map/reduce_scatter | solution.py:51
  557.0 170.2 %copy-start.5 = (f32[256,768]{1,0:T(8,128)S(1)}, f32[256,768]{1,0:T(8,128)}, u32[]{:S(2)}) copy-start(f32[256,768]{1,0:T(8,128)} %copy-done.4) | copy-start | bytes 2359300
  700.2 31.8 %all-to-all-start.9 = ((bf16[4,1,24]{2,1,0:T(2,128)(2,1)}), bf16[4,1,24]{2,1,0:T(2,128)(2,1)S(1)}, u32[]{:S(2)}, u32[]{:S(2)}) async-start(bf16[4,1,24]{2,1,0:T(2,128)(2,1)} %broadcast_in_dim.107), calls=%async_computation.11 | async-start | bytes 4096 | tf_op jit(solution)/shard_map/all_to_all | solution.py:60
  732.6 8.8 %all-to-all-start.10 = ((bf16[4,1,24]{2,1,0:T(2,128)(2,1)}), bf16[4,1,24]{2,1,0:T(2,128)(2,1)S(1)}, u32[]{:S(2)}, u32[]{:S(2)}) async-start(bf16[4,1,24]{2,1,0:T(2,128)(2,1)} %broadcast_in_dim.108), calls=%async_computation.12 | async-start | bytes 4096 | tf_op jit(solution)/shard_map/all_to_all | solution.py:60
  742.0 8.4 all-to-all-start.11
  751.0 8.0 all-to-all-start.12
  759.6 8.8 %all-to-all-start.13 = ((bf16[4,1,24]{2,1,0:T(2,128)(2,1)}), bf16[4,1,24]{2,1,0:T(2,128)(2,1)S(1)}, u32[]{:S(2)}, u32[]{:S(2)}) async-start(bf16[4,1,24]{2,1,0:T(2,128)(2,1)} %broadcast_in_dim.111), calls=%async_computation.15 | async-start | bytes 4096 | tf_op jit(solution)/shard_map/all_to_all | solution.py:60
  769.0 8.4 all-to-all-start.15
  778.0 8.0 all-to-all-start.16
  786.6 8.8 %all-to-all-start.17 = ((bf16[4,1,24]{2,1,0:T(2,128)(2,1)}), bf16[4,1,24]{2,1,0:T(2,128)(2,1)S(1)}, u32[]{:S(2)}, u32[]{:S(2)}) async-start(bf16[4,1,24]{2,1,0:T(2,128)(2,1)} %broadcast_in_dim.115), calls=%async_computation.19 | async-start | bytes 4096 | tf_op jit(solution)/shard_map/all_to_all | solution.py:60
  796.0 8.4 all-to-all-start.14
  806.2 13.8 %all-to-all-start.8 = ((bf16[4,96,768]{2,1,0:T(8,128)(2,1)}), bf16[4,96,768]{2,1,0:T(8,128)(2,1)S(1)}, u32[]{:S(2)}, u32[]{:S(2)}) async-start(bf16[4,96,768]{2,1,0:T(8,128)(2,1)} %broadcast_in_dim.106), calls=%async_computation.10 | async-start | bytes 1179648 | tf_op jit(solution)/shard_map/all_to_all | solution.py:60
  820.6 9.5 %all-to-all-start.6 = ((bf16[4,24,768]{2,1,0:T(8,128)(2,1)}), bf16[4,24,768]{2,1,0:T(8,128)(2,1)S(1)}, u32[]{:S(2)}, u32[]{:S(2)}) async-start(bf16[4,24,768]{2,1,0:T(8,128)(2,1)} %broadcast_in_dim.104), calls=%async_computation.7 | async-start | bytes 294912 | tf_op jit(solution)/shard_map/all_to_all | solution.py:60
  830.9 13.0 %all-to-all-start.5 = ((bf16[4,24,2304]{2,1,0:T(8,128)(2,1)}), bf16[4,24,2304]{2,1,0:T(8,128)(2,1)S(1)}, u32[]{:S(2)}, u32[]{:S(2)}) async-start(bf16[4,24,2304]{2,1,0:T(8,128)(2,1)} %broadcast_in_dim.103), calls=%async_computation.6 | async-start | bytes 884736 | tf_op jit(solution)/shard_map/all_to_all | solution.py:60
  844.7 14.5 %all-to-all-start.7 = ((bf16[4,24,3072]{2,1,0:T(8,128)(2,1)}), bf16[4,24,3072]{2,1,0:T(8,128)(2,1)S(1)}, u32[]{:S(2)}, u32[]{:S(2)}) async-start(bf16[4,24,3072]{2,1,0:T(8,128)(2,1)} %broadcast_in_dim.105), calls=%async_computation.8 | async-start | bytes 1179648 | tf_op jit(solution)/shard_map/all_to_all | solution.py:60
  (46 other events, 406.7 us)
Sparse Core Ops, SparseCore 0:
  10.2 220.1 all-gather.2
  232.1 154.9 all-gather.4
  397.6 182.2 reduce-scatter.4
  582.2 234.3 reduce-scatter.2
where the time goes:
time: 874 us; the launch traced here: 867 us
  blocking collectives  291 us (33%)
  waiting for transfers between devices  277 us (32%)
  starting transfers between devices  110 us (13%)
  matrix products  69.5 us (8%)
  local copies, waits for them, and re-layouts  61.1 us (7%)
  other arithmetic  33.9 us (4%)
  between operations  17.8 us (2%)
    unnamed x2, blocking collectives  285 us
    all_to_all x13, starting transfers between devices, sent_to_all(): return lax.all_to_all(copies, axis, split_axis=0, concat_axis=0, tiled=True)  73 us
    all_gather x1, waiting for transfers between devices, in_one_piece(): filled = lax.all_gather(both, axis, axis=dim, tiled=True)  66.4 us
    all_gather x1, waiting for transfers between devices, body(): lax.all_gather(w_back, 'fsdp', axis=0, tiled=True)  59 us
    all_to_all x13, waiting for transfers between devices, sent_to_all(): return lax.all_to_all(copies, axis, split_axis=0, concat_axis=0, tiled=True)  57.7 us
    all_to_all x1, waiting for transfers between devices, body(): lax.all_to_all(stacked, SP, split_axis=0, concat_axis=2, tiled=True)  39.6 us
    all_to_all x1, waiting for transfers between devices, turned_blocks(): lax.all_to_all(blocks, axes[k], split_axis=k, concat_axis=k, tiled=True)  29.1 us
    all_to_all x1, starting transfers between devices, body(): lax.all_to_all(d_ctx.reshape(rows, groups, span), SP, split_axis=1, conca...  21.6 us
  transfers between devices with their start and end apart: 21, of which 20 were waited for; matrix products, arithmetic and copies ran while one was open for 17% of the time, Pallas kernels for 0%

commit v1 on v0

v1 whole, which is shorter than its diff:
```python
import jax
import jax.numpy as jnp
from jax import lax
from jax.sharding import Mesh
from jax.sharding import PartitionSpec as P

H = 12
HD = 64
FSDP = "fsdp"
SP = ("sp_0", "sp_1")
FSDP_SP = ("fsdp", "sp_0", "sp_1")
EPS = 1e-05
BF = jnp.bfloat16
F32 = jnp.float32


def swap_core(value):
    return lax.ppermute(value, "sp_1", [(0, 1), (1, 0)])


def swap_chip(value):
    return lax.ppermute(value, "sp_0", [(0, 1), (1, 0)])


def swap_both(value):
    return lax.ppermute(value, SP, [(0, 3), (1, 2), (2, 1), (3, 0)])


def gather_relative(value):
    across = swap_chip(value)
    return [value, swap_core(value), across, swap_core(across)]


def gather_direct(value):
    return [value, swap_core(value), swap_chip(value), swap_both(value)]


def exchange_direct(parts):
    return [parts[0], swap_core(parts[1]), swap_chip(parts[2]), swap_both(parts[3])]


def reduce_relative(parts):
    far = parts[2] + swap_core(parts[3].astype(BF)).astype(F32)
    far = swap_chip(far.astype(BF)).astype(F32)
    near = parts[0] + swap_core(parts[1].astype(BF)).astype(F32)
    return near + far


def reorder(parts):
    chip = lax.axis_index("sp_0") == 1
    core = lax.axis_index("sp_1") == 1
    a, b, c, d = parts
    a, b, c, d = (
        jnp.where(core, b, a),
        jnp.where(core, a, b),
        jnp.where(core, d, c),
        jnp.where(core, c, d),
    )
    return [
        jnp.where(chip, c, a),
        jnp.where(chip, d, b),
        jnp.where(chip, a, c),
        jnp.where(chip, b, d),
    ]


def spread(value):
    copies = jnp.broadcast_to(value, (lax.axis_size(FSDP), *value.shape))
    filled = lax.all_to_all(copies, FSDP, split_axis=0, concat_axis=0, tiled=True)
    return filled.reshape(-1, value.shape[-1])


def collect(value):
    count = lax.axis_size(FSDP)
    blocks = value.reshape(count, value.shape[0] // count, value.shape[1])
    blocks = lax.all_to_all(blocks, FSDP, split_axis=0, concat_axis=0, tiled=True)
    return blocks.astype(F32).sum(axis=0)


def layer_norm(hidden, gain, shift):
    mean = jnp.mean(hidden, axis=-1, keepdims=True)
    centred = hidden - mean
    variance = jnp.mean(centred * centred, axis=-1, keepdims=True)
    inverse = lax.rsqrt(variance + EPS)
    normed = centred * inverse
    return (normed * gain + shift, normed, inverse)


def norm_back(grad, normed, inverse, gain):
    scaled = grad * gain
    first = jnp.mean(scaled, axis=-1, keepdims=True)
    second = jnp.mean(scaled * normed, axis=-1, keepdims=True)
    return inverse * (scaled - first - normed * second)


def gelu_exact(value):
    return jax.nn.gelu(value, approximate=False)


def dot(left, right):
    return jnp.dot(left, right, preferred_element_type=F32)


def contract_rows(left, right):
    return lax.dot_general(left, right, (((0,), (0,)), ((), ())), preferred_element_type=F32)


def contract_cols(left, right):
    return lax.dot_general(left, right, (((1,), (1,)), ((), ())), preferred_element_type=F32)


def attend_heads(query, keys, values, valid, scale):
    scores = jnp.einsum("qhd,khd->hqk", query, keys, preferred_element_type=F32) * scale
    scores = jnp.where(valid[None, None, :], scores, -jnp.inf)
    top = jnp.max(scores, axis=-1, keepdims=True)
    expo = jnp.exp(scores - top)
    summed = jnp.sum(expo, axis=-1, keepdims=True)
    probs = (expo / summed).astype(BF)
    context = jnp.einsum("hqk,khd->qhd", probs, values, preferred_element_type=F32).astype(BF)
    return (context, (top + jnp.log(summed))[..., 0])


def attend_back(query, keys, values, context, logsum, grads, valid, scale):
    scores = jnp.einsum("qhd,khd->hqk", query, keys, preferred_element_type=F32) * scale
    scores = jnp.where(valid[None, None, :], scores, -jnp.inf)
    probs = jnp.exp(scores - logsum[..., None])
    probs_b = probs.astype(BF)
    grad_values = jnp.einsum("hqk,qhd->khd", probs_b, grads, preferred_element_type=F32)
    grad_probs = jnp.einsum("qhd,khd->hqk", grads, values, preferred_element_type=F32)
    delta = jnp.sum(grads.astype(F32) * context.astype(F32), axis=-1).T
    grad_scores = (probs * (grad_probs - delta[..., None])).astype(BF)
    grad_query = jnp.einsum("hqk,khd->qhd", grad_scores, keys, preferred_element_type=F32) * scale
    grad_keys = jnp.einsum("hqk,qhd->khd", grad_scores, query, preferred_element_type=F32) * scale
    return (grad_query.astype(BF), grad_keys.astype(BF), grad_values.astype(BF))


def body(
    tokens,
    lengths,
    w_qkv,
    w_out,
    w_in,
    w_back,
    bias_q,
    bias_v,
    bias_o,
    gain_one,
    shift_one,
    bias_in,
    bias_back,
    gain_two,
    shift_two,
    cotangent,
):
    rows, width = tokens.shape
    members = lax.axis_size(SP)
    shards = lax.axis_size(FSDP)
    local = H // members
    span = local * HD
    total = rows * members
    scale = HD ** (-0.5)
    depth = w_qkv.shape[0]
    piece = w_back.shape[0] // members
    hidden = piece * shards
    me = lax.axis_index("sp_0") * 2 + lax.axis_index("sp_1")

    mine_qkv = lax.dynamic_index_in_dim(w_qkv.reshape(depth, 3, members, span), me, 2, False)
    mine_in = lax.dynamic_index_in_dim(w_in.reshape(depth, shards, members, piece), me, 2, False)
    mine_back = lax.dynamic_index_in_dim(w_back.reshape(members, piece, width), me, 0, False)
    mine_bias = lax.dynamic_index_in_dim(bias_in.reshape(members, piece), me, 0, False)
    vectors = jnp.stack(
        [bias_q, bias_v, bias_o, gain_one, shift_one, bias_back, gain_two, shift_two, mine_bias],
        axis=1,
    )
    vectors = jnp.pad(vectors, ((0, 0), (0, 64 - vectors.shape[1])))
    first = spread(jnp.concatenate([mine_qkv.reshape(depth, 3 * span), vectors], axis=1))
    second = spread(
        jnp.concatenate([w_out, mine_in.reshape(depth, hidden), mine_back], axis=1)
    )
    w_qkv_m = first[:, : 3 * span]
    small = first[:, 3 * span :].astype(F32).T
    b_q, b_v, b_o, g_one, s_one, b_back, g_two, s_two, b_in = [small[k] for k in range(9)]
    w_out_all = second[:, :width]
    w_in_m = second[:, width : width + hidden]
    w_back_m = second[:, width + hidden :]

    x_all = jnp.concatenate(gather_relative(tokens), axis=0)
    own_q = lax.dynamic_slice_in_dim(b_q, me * span, span, 0)
    own_v = lax.dynamic_slice_in_dim(b_v, me * span, span, 0)
    bias_qkv = jnp.concatenate([own_q, jnp.zeros((span,), F32), own_v])
    packed = (dot(x_all, w_qkv_m) + bias_qkv).astype(BF)
    query, keys, values = [
        packed[:, k * span : (k + 1) * span].reshape(total, local, HD) for k in range(3)
    ]
    place = jnp.arange(members, dtype=jnp.int32) ^ me
    position = (place[:, None] * rows + jnp.arange(rows, dtype=jnp.int32)).reshape(total)
    valid = position < lengths[0]
    context, logsum = attend_heads(query, keys, values, valid, scale)

    parts = context.reshape(members, rows, span)
    ctx_rows = jnp.concatenate(
        reorder(exchange_direct([parts[m] for m in range(members)])), axis=1
    )
    h_one = tokens.astype(F32) + dot(ctx_rows, w_out_all) + b_o
    y_one, n_one, i_one = layer_norm(h_one, g_one, s_one)
    y_oneb = y_one.astype(BF)
    y_all = jnp.concatenate(gather_relative(y_oneb), axis=0)
    pre = dot(y_all, w_in_m) + b_in
    act = gelu_exact(pre).astype(BF)
    partial = dot(act, w_back_m).reshape(members, rows, width)
    h_two = y_oneb.astype(F32) + b_back + reduce_relative(partial)
    out, n_two, i_two = layer_norm(h_two, g_two, s_two)

    grad = cotangent.astype(F32)
    d_g2 = jnp.sum(grad * n_two, axis=0)
    d_s2 = jnp.sum(grad, axis=0)
    dh_two = norm_back(grad, n_two, i_two, g_two)
    d_bb = jnp.sum(dh_two, axis=0)
    dh_all = jnp.concatenate(gather_relative(dh_two.astype(BF)), axis=0)
    d_act = contract_cols(dh_all, w_back_m)
    d_pre = jax.vjp(gelu_exact, pre)[1](d_act)[0]
    d_preb = d_pre.astype(BF)
    back = contract_cols(d_preb, w_in_m).reshape(members, rows, width)
    dy_one = dh_two + reduce_relative(back)
    d_bi = jnp.sum(d_pre, axis=0)
    d_wb = contract_rows(act, dh_all)
    d_wi = contract_rows(y_all, d_preb)

    d_g1 = jnp.sum(dy_one * n_one, axis=0)
    d_s1 = jnp.sum(dy_one, axis=0)
    dh_one = norm_back(dy_one, n_one, i_one, g_one)
    d_bo = jnp.sum(dh_one, axis=0)
    dh_oneb = dh_one.astype(BF)
    d_ctx = contract_cols(dh_oneb, w_out_all).astype(BF)
    pieces = exchange_direct(reorder([d_ctx[:, m * span : (m + 1) * span] for m in range(members)]))
    grad_heads = jnp.concatenate(pieces, axis=0).reshape(total, local, HD)

    columns = reorder([dh_oneb[:, m * span : (m + 1) * span] for m in range(members)])
    d_wo = reduce_relative([contract_rows(ctx_rows, column) for column in columns])
    early = collect(jnp.concatenate([d_wo.astype(BF), d_wi.astype(BF), d_wb.astype(BF)], axis=1))
    early = reorder(gather_direct(early))

    g_query, g_keys, g_values = attend_back(
        query, keys, values, context, logsum, grad_heads, valid, scale
    )
    d_packed = jnp.concatenate(
        [g.reshape(total, span) for g in (g_query, g_keys, g_values)], axis=1
    )
    d_x = dh_one + reduce_relative(contract_cols(d_packed, w_qkv_m).reshape(members, rows, width))
    d_wq = contract_rows(x_all, d_packed)
    empty = jnp.zeros((width,), F32)
    own = jnp.sum(d_packed.astype(F32), axis=0)
    d_bq = lax.dynamic_update_slice_in_dim(empty, own[:span], me * span, 0)
    d_bv = lax.dynamic_update_slice_in_dim(empty, own[2 * span :], me * span, 0)
    sums = jnp.stack([d_bq, d_bv, d_bo, d_g1, d_s1, d_bb, d_g2, d_s2, d_bi], axis=1)
    sums = jnp.pad(sums, ((0, 0), (0, 64 - sums.shape[1])))
    late = collect(jnp.concatenate([d_wq, sums], axis=1).astype(BF))
    late = reorder(gather_direct(late))

    grad_qkv = (
        jnp.stack([part[:, : 3 * span].reshape(depth, 3, span) for part in late], axis=2)
    ).reshape(depth, 3 * width)
    grad_out = jnp.concatenate([part[:, :span] for part in early], axis=1)
    grad_in = jnp.stack(
        [part[:, span : span + hidden].reshape(depth, shards, piece) for part in early], axis=2
    ).reshape(depth, members * hidden)
    grad_back = jnp.concatenate([part[:, span + hidden :] for part in early], axis=0)
    tails = [part[:, 3 * span : 3 * span + 9].T for part in late]
    summed = tails[0] + tails[1] + tails[2] + tails[3]
    grad_bias_in = jnp.concatenate([tail[8] for tail in tails])
    return (
        out.astype(BF),
        d_x.astype(BF),
        grad_qkv,
        grad_out,
        grad_in,
        grad_back,
        summed[0],
        summed[1],
        summed[2],
        summed[3],
        summed[4],
        grad_bias_in,
        summed[5],
        summed[6],
        summed[7],
    )


def solution(mesh):
    split = Mesh(mesh.devices.reshape(mesh.shape["fsdp"], 2, 2), FSDP_SP)
    rows, flat = P("fsdp", None), P("fsdp")
    both = P(FSDP_SP, None)
    in_specs = (both, flat, rows, rows, rows, rows, *(flat,) * 9, both)
    out_specs = (both, both, rows, rows, rows, rows, *(flat,) * 9)
    return jax.shard_map(body, mesh=split, in_specs=in_specs, out_specs=out_specs, check_vma=False)
```

time: 874 us -> 333 us (0.38)
  blocking collectives: 291 us -> 0 us
  waiting for transfers between devices: 277 us -> 116 us
  starting transfers between devices: 110 us -> 70.1 us
  local copies, waits for them, and re-layouts: 61.1 us -> 45 us
  between operations: 17.8 us -> 3.03 us
  other arithmetic: 33.9 us -> 23.3 us
    unnamed x2 -> x0, blocking collectives: 285 us -> none
    all_to_all x17 -> x4, waiting for transfers between devices: 147 us -> 8.83 us  [the longest x2 8.82 us: spread(): lax.all_to_all(copies, FSDP, split_axis=0, concat_axis=0, tiled=True)]
    all_gather x2 -> x0, waiting for transfers between devices: 125 us -> none  [the longest x1 66.4 us: in_one_piece(): filled = lax.all_gather(both, axis, axis=dim, tiled=True)]
    ppermute x0 -> x33, waiting for transfers between devices: none -> 108 us  [the longest x11 66.5 us: swap_chip(): return lax.ppermute(value, 'sp_0', [(0, 1), (1, 0)])]
    all_to_all x17 -> x4, starting transfers between devices: 110 us -> 26.2 us  [the longest x2 13.1 us: spread(): lax.all_to_all(copies, FSDP, split_axis=0, concat_axis=0, tiled=True)]
    ppermute x0 -> x33, starting transfers between devices: none -> 43.8 us  [the longest x18 17.8 us: swap_core(): return lax.ppermute(value, 'sp_1', [(0, 1), (1, 0)])]
    another operation x8 -> x30, local copies, waits for them, and re-layouts: 5.38 us -> 15.7 us  [the longest x11 6.19 us: body(): jnp.stack([bias_q, bias_v, bias_o, gain_one, shift_one, bias_back, gain_t...]
    all_to_all x8 -> x0, local copies, waits for them, and re-layouts: 10.1 us -> none  [the longest x2 4.06 us: body(): lax.all_to_all(stacked, SP, split_axis=0, concat_axis=2, tiled=True)]
  transfers between devices with their start and end apart: 21 -> 37, of which waited for: 20 -> 15; matrix products, arithmetic and copies ran while one was open for 17% -> 28% of each run, Pallas kernels for 0% -> 0%
where the time goes in v1:
time: 333 us; the launch traced here: 327 us
  waiting for transfers between devices  116 us (35%)
  starting transfers between devices  70.1 us (21%)
  matrix products  69.7 us (21%)
  local copies, waits for them, and re-layouts  45 us (14%)
  other arithmetic  23.3 us (7%)
    ppermute x11, waiting for transfers between devices, swap_chip(): return lax.ppermute(value, 'sp_0', [(0, 1), (1, 0)])  66.5 us
    ppermute x4, waiting for transfers between devices, swap_both(): return lax.ppermute(value, SP, [(0, 3), (1, 2), (2, 1), (3, 0)])  37.2 us
    ppermute x18, starting transfers between devices, swap_core(): return lax.ppermute(value, 'sp_1', [(0, 1), (1, 0)])  17.8 us
    ppermute x11, starting transfers between devices, swap_chip(): return lax.ppermute(value, 'sp_0', [(0, 1), (1, 0)])  16.9 us
    dot_general x4, matrix products, dot(): return jnp.dot(left, right, preferred_element_type=F32)  16.6 us
    dot_general x4, matrix products, contract_cols(): lax.dot_general(left, right, (((1,), (1,)), ((), ())), preferred_element_...  15.9 us
    dot_general x7, matrix products, contract_rows(): lax.dot_general(left, right, (((0,), (0,)), ((), ())), preferred_element_...  13.6 us
    all_to_all x2, starting transfers between devices, spread(): lax.all_to_all(copies, FSDP, split_axis=0, concat_axis=0, tiled=True)  13.1 us
  transfers between devices with their start and end apart: 37, of which 15 were waited for; matrix products, arithmetic and copies ran while one was open for 28% of the time, Pallas kernels for 0%

profile of v1, /device:TPU:1, one launch (start us, length us, event | category | flops | bytes accessed | tf_op | source)
XLA Modules:
  0.0 327.4 jit_solution(10118977031063695125)
XLA Ops:
  14.5 8.1 %all-to-all-start = ((bf16[32,24,640]{2,1,0:T(8,128)(2,1)}), bf16[32,24,640]{2,1,0:T(8,128)(2,1)S(1)}, u32[]{:S(2)}, u32[]{:S(2)}) async-start(bf16[32,24,640]{2,1,0:T(8,128)(2,1)} %broadcast_in_dim.24), calls=%async_computation | async-start | bytes 1966080 | tf_op jit(solution)/shard_map/all_to_all | solution.py:69
  30.0 8.8 %all-to-all-done = bf16[32,24,640]{2,1,0:T(8,128)(2,1)S(1)} async-done(((bf16[32,24,640]{2,1,0:T(8,128)(2,1)}), bf16[32,24,640]{2,1,0:T(8,128)(2,1)S(1)}, u32[]{:S(2)}, u32[]{:S(2)}) %all-to-all-start) | async-done | bytes 983072 | tf_op jit(solution)/shard_map/all_to_all | solution.py:69
  40.9 5.1 %all-to-all-start.1 = ((bf16[32,24,2304]{2,1,0:T(8,128)(2,1)}), bf16[32,24,2304]{2,1,0:T(8,128)(2,1)}, u32[]{:S(2)}, u32[]{:S(2)}) async-start(bf16[32,24,2304]{2,1,0:T(8,128)(2,1)} %broadcast_in_dim.48), calls=%async_computation.1 | async-start | bytes 7077888 | tf_op jit(solution)/shard_map/all_to_all | solution.py:69
  58.3 3.2 fusion.23
  61.9 3.5 %collective-permute-start.3 = (bf16[256,192]{1,0:T(8,128)(2,1)S(1)}, bf16[256,192]{1,0:T(8,128)(2,1)S(1)}, u32[]{:S(2)}, u32[]{:S(2)}) collective-permute-start(bf16[256,192]{1,0:T(8,128)(2,1)S(1)} %copy.198), channel_id=1, source_target_pairs={{0,3},{1,2},{2,1},{3,0},{4,7},{5,6},{6,5},{7,4},{8,11},{9,10},{10,... | collective-permute-start | bytes 294920 | tf_op jit(solution)/shard_map/ppermute | solution.py:26
  66.7 27.2 %collective-permute-done.3 = bf16[256,192]{1,0:T(8,128)(2,1)S(1)} collective-permute-done((bf16[256,192]{1,0:T(8,128)(2,1)S(1)}, bf16[256,192]{1,0:T(8,128)(2,1)S(1)}, u32[]{:S(2)}, u32[]{:S(2)}) %collective-permute-start.3) | collective-permute-done | bytes 98336 | tf_op jit(solution)/shard_map/ppermute | solution.py:26
  100.9 6.8 %collective-permute-done.7 = bf16[256,768]{1,0:T(8,128)(2,1)S(1)} collective-permute-done((bf16[256,768]{1,0:T(8,128)(2,1)S(1)}, bf16[256,768]{1,0:T(8,128)(2,1)S(1)}, u32[]{:S(2)}, u32[]{:S(2)}) %collective-permute-start.7) | collective-permute-done | bytes 393248 | tf_op jit(solution)/shard_map/ppermute | solution.py:22
  112.0 8.9 %multiply_convert_fusion.1 = (bf16[1024,768]{1,0:T(8,128)(2,1)S(1)}, f32[1024,768]{1,0:T(8,128)S(1)}, f32[1024,768]{1,0:T(8,128)S(1)}) fusion(f32[768]{0:T(1024)S(1)} %copy-done.46, bf16[768,2304]{1,0:T(8,128)(2,1)} %bitcast.22, bf16[256,768]{1,0:T(8,128)(2,1)S(1)} %collective-permute-done.8, bf16[256,768]{1,0:T(8,128)(2,1)S(1)} %collective-permute-done.7, ...), kind=kOutput, calls=%fused_computation.15 | convolution fusion | flops 1266155520 | bytes 10619904 | tf_op jit(solution)/shard_map/dot_general | solution.py:101
  120.9 3.2 fusion.95
  127.6 10.6 %collective-permute-done.11 = bf16[256,768]{1,0:T(8,128)(2,1)S(1)} collective-permute-done((bf16[256,768]{1,0:T(8,128)(2,1)S(1)}, bf16[256,768]{1,0:T(8,128)(2,1)S(1)}, u32[]{:S(2)}, u32[]{:S(2)}) %collective-permute-start.11) | collective-permute-done | bytes 393248 | tf_op jit(solution)/shard_map/ppermute | solution.py:22
  143.3 8.2 %collective-permute-done.13 = bf16[256,768]{1,0:T(8,128)(2,1)S(1)} collective-permute-done((bf16[256,768]{1,0:T(8,128)(2,1)S(1)}, bf16[256,768]{1,0:T(8,128)(2,1)S(1)}, u32[]{:S(2)}, u32[]{:S(2)}) %collective-permute-start.13) | collective-permute-done | bytes 393248 | tf_op jit(solution)/shard_map/ppermute | solution.py:22
  155.1 5.3 %fusion.98 = (bf16[768]{0:T(1024)(128)(2,1)S(1)}, bf16[1024,768]{1,0:T(8,128)(2,1)S(1)}) fusion(f32[1024,768]{1,0:T(8,128)S(1)} %get-tuple-element.45, bf16[768,2304]{1,0:T(8,128)(2,1)} %bitcast.22, bf16[256,768]{1,0:T(8,128)(2,1)S(1)} %collective-permute-done.14, bf16[256,768]{1,0:T(8,128)(2,1)S(1)} %collective-permute-done.13, ...), kind=kOutput, calls=%fused_computation.236 | convolution fusion | flops 1226833152 | bytes 10621440 | tf_op jit(solution)/shard_map/dot_general | solution.py:109
  160.4 4.9 %fusion.96 = (bf16[1024,768]{1,0:T(8,128)(2,1)S(1)}, f32[1024,768]{1,0:T(8,128)}) fusion(bf16[768,2304]{1,0:T(8,128)(2,1)} %bitcast.22, bf16[1024,768]{1,0:T(8,128)(2,1)S(1)} %get-tuple-element.100), kind=kOutput, calls=%fused_computation.234 | convolution fusion | flops 1208745984 | bytes 7471104 | tf_op jit(solution)/shard_map/dot_general | solution.py:109
  172.5 4.3 %convolution_convert_fusion = bf16[768,768]{0,1:T(8,128)(2,1)} fusion(bf16[1024,768]{1,0:T(8,128)(2,1)} %copy-done.56, bf16[256,768]{1,0:T(8,128)(2,1)} %copy-done.55, bf16[256,768]{1,0:T(8,128)(2,1)} %copy-done.53, bf16[256,768]{1,0:T(8,128)(2,1)} %copy-done.54, bf16[256,768]{1,0:T(8,128)(2,1)} %copy-done.17), kind=kOutput, calls=%fused_computation.36 | convolution fusion | flops 1214840832 | bytes 4325376 | tf_op jit(solution)/shard_map/dot_general | solution.py:105
  176.8 6.3 %collective-permute-done.17 = bf16[256,768]{1,0:T(8,128)(2,1)S(1)} collective-permute-done((bf16[256,768]{1,0:T(8,128)(2,1)S(1)}, bf16[256,768]{1,0:T(8,128)(2,1)S(1)}, u32[]{:S(2)}, u32[]{:S(2)}) %collective-permute-start.17) | collective-permute-done | bytes 393248 | tf_op jit(solution)/shard_map/ppermute | solution.py:22
  200.0 7.7 %fusion.14 = bf16[3,64,1024]{2,1,0:T(8,128)(2,1)S(1)} fusion(bf16[1024,3,64]{0,2,1:T(8,128)(2,1)S(1)} %bitcast.94, f32[3,1024,1024]{1,2,0:T(8,128)} %copy-done.2, f32[3,1024]{1,0:T(4,128)S(1)} %copy-done.36, pred[1024]{0:T(1024)(128)(4,1)} %copy-done.37), kind=kOutput, calls=%fused_computation.43 | convolution fusion | flops 415432704 | bytes 13382656 | tf_op jit(solution)/shard_map/hqk,qhd->khd/dot_general | solution.py:128
  207.6 7.0 %multiply_convert_fusion = bf16[3,1024,1024]{1,2,0:T(8,128)(2,1)S(1)} fusion(f32[3,1024,1024]{1,2,0:T(8,128)} %copy-done.2, f32[3,1024]{1,0:T(4,128)S(1)} %bitcast.113, f32[3,1024]{1,0:T(4,128)S(1)} %copy-done.36, pred[1024]{0:T(1024)(128)(4,1)S(1)} %copy-done.38, bf16[1024,3,64]{0,2,1:T(8,128)(2,1)S(1)} %bitcast.95, bf16[1024,3,64]{0,2,1:T(8,128)(2,1)S(1)} %bitcast.101), kind=kOutput, calls=%fused_computation | convolution fusion | flops 421527552 | bytes 19686400 | tf_op jit(solution)/shard_map/qhd,khd->hqk/dot_general | solution.py:129
  220.8 3.6 %fusion.97 = (bf16[1024,768]{1,0:T(8,128)(2,1)}, f32[1024,768]{1,0:T(8,128)}) fusion(bf16[768,640]{1,0:T(8,128)(2,1)S(1)} %bitcast.98, bf16[1024,192]{0,1:T(8,128)(2,1)S(1)} %bitcast.108, bf16[1024,192]{0,1:T(8,128)(2,1)S(1)} %bitcast.89, bf16[1024,192]{0,1:T(8,128)(2,1)S(1)} %bitcast.92), kind=kOutput, calls=%fused_computation.235 | convolution fusion | flops 910295040 | bytes 6881280 | tf_op jit(solution)/shard_map/dot_general | solution.py:109
  229.2 6.3 %all-to-all-start.2 = ((bf16[32,24,640]{2,1,0:T(8,128)(2,1)}), bf16[32,24,640]{2,1,0:T(8,128)(2,1)}, u32[]{:S(2)}, u32[]{:S(2)}) async-start(bf16[32,24,640]{2,1,0:T(8,128)(2,1)} %pad_maximum_fusion.5), calls=%async_computation.2 | async-start | bytes 1966080 | tf_op jit(solution)/shard_map/all_to_all | solution.py:76
  245.5 9.9 %collective-permute-done.29 = bf16[768,192]{0,1:T(8,128)(2,1)S(1)} collective-permute-done((bf16[768,192]{0,1:T(8,128)(2,1)S(1)}, bf16[768,192]{0,1:T(8,128)(2,1)S(1)}, u32[]{:S(2)}, u32[]{:S(2)}) %collective-permute-start.29) | collective-permute-done | bytes 294944 | tf_op jit(solution)/shard_map/ppermute | solution.py:22
  257.0 4.2 %copy.217 = bf16[768,1728]{1,0:T(8,128)(2,1)} copy(bf16[768,1728]{0,1:T(8,128)(2,1)S(1)} %pad_maximum_fusion) | data formatting | bytes 5308416 | tf_op jit(solution)/shard_map/concatenate | solution.py:240
  261.2 6.8 %all-to-all-start.3 = ((bf16[32,24,1728]{2,1,0:T(8,128)(2,1)}), bf16[32,24,1728]{2,1,0:T(8,128)(2,1)S(1)}, u32[]{:S(2)}, u32[]{:S(2)}) async-start(bf16[32,24,1728]{2,1,0:T(8,128)(2,1)} %bitcast.35), calls=%async_computation.3 | async-start | bytes 5505024 | tf_op jit(solution)/shard_map/all_to_all | solution.py:76
  277.3 23.7 %collective-permute-done.25 = f32[24,640]{1,0:T(8,128)S(1)} collective-permute-done((f32[24,640]{1,0:T(8,128)S(1)}, f32[24,640]{1,0:T(8,128)S(1)}, u32[]{:S(2)}, u32[]{:S(2)}) %collective-permute-start.25) | collective-permute-done | bytes 61472 | tf_op jit(solution)/shard_map/ppermute | solution.py:22
  315.7 4.3 %collective-permute-done.30 = f32[24,1728]{1,0:T(8,128)S(1)} collective-permute-done((f32[24,1728]{1,0:T(8,128)S(1)}, f32[24,1728]{1,0:T(8,128)S(1)}, u32[]{:S(2)}, u32[]{:S(2)}) %collective-permute-start.30) | collective-permute-done | bytes 165920 | tf_op jit(solution)/shard_map/ppermute | solution.py:26
  (322 shorter events, 136.6 us)
Async XLA Ops:
  0.7 27.0 %collective-permute-start = (bf16[256,768]{1,0:T(8,128)(2,1)}, bf16[256,768]{1,0:T(8,128)(2,1)S(1)}, u32[]{:S(2)}, u32[]{:S(2)}) collective-permute-start(bf16[256,768]{1,0:T(8,128)(2,1)} %param.16), channel_id=1, source_target_pairs={{0,1},{1,0},{2,3},{3,2},{4,5},{5,4},{6,7},{7,6},{8,9},{9,8},{10,11... | collective-permute-start | bytes 1179656 | tf_op jit(solution)/shard_map/ppermute | solution.py:18
  2.2 23.9 %collective-permute-start.1 = (bf16[256,768]{1,0:T(8,128)(2,1)}, bf16[256,768]{1,0:T(8,128)(2,1)S(1)}, u32[]{:S(2)}, u32[]{:S(2)}) collective-permute-start(bf16[256,768]{1,0:T(8,128)(2,1)} %param.16), channel_id=1, source_target_pairs={{0,2},{2,0},{1,3},{3,1},{4,6},{6,4},{5,7},{7,5},{8,10},{10,8},{9,1... | collective-permute-start | bytes 1179656 | tf_op jit(solution)/shard_map/ppermute | solution.py:22
  14.5 24.4 %all-to-all-start = ((bf16[32,24,640]{2,1,0:T(8,128)(2,1)}), bf16[32,24,640]{2,1,0:T(8,128)(2,1)S(1)}, u32[]{:S(2)}, u32[]{:S(2)}) async-start(bf16[32,24,640]{2,1,0:T(8,128)(2,1)} %broadcast_in_dim.24), calls=%async_computation | async-start | bytes 1966080 | tf_op jit(solution)/shard_map/all_to_all | solution.py:69
  40.9 53.1 %all-to-all-start.1 = ((bf16[32,24,2304]{2,1,0:T(8,128)(2,1)}), bf16[32,24,2304]{2,1,0:T(8,128)(2,1)}, u32[]{:S(2)}, u32[]{:S(2)}) async-start(bf16[32,24,2304]{2,1,0:T(8,128)(2,1)} %broadcast_in_dim.48), calls=%async_computation.1 | async-start | bytes 7077888 | tf_op jit(solution)/shard_map/all_to_all | solution.py:69
  61.9 32.0 %collective-permute-start.3 = (bf16[256,192]{1,0:T(8,128)(2,1)S(1)}, bf16[256,192]{1,0:T(8,128)(2,1)S(1)}, u32[]{:S(2)}, u32[]{:S(2)}) collective-permute-start(bf16[256,192]{1,0:T(8,128)(2,1)S(1)} %copy.198), channel_id=1, source_target_pairs={{0,3},{1,2},{2,1},{3,0},{4,7},{5,6},{6,5},{7,4},{8,11},{9,10},{10,... | collective-permute-start | bytes 294920 | tf_op jit(solution)/shard_map/ppermute | solution.py:26
  65.4 28.5 %collective-permute-start.4 = (bf16[256,192]{1,0:T(8,128)(2,1)S(1)}, bf16[256,192]{1,0:T(8,128)(2,1)S(1)}, u32[]{:S(2)}, u32[]{:S(2)}) collective-permute-start(bf16[256,192]{1,0:T(8,128)(2,1)S(1)} %copy.199), channel_id=1, source_target_pairs={{0,2},{2,0},{1,3},{3,1},{4,6},{6,4},{5,7},{7,5},{8,10},{10,8},{9,1... | collective-permute-start | bytes 294920 | tf_op jit(solution)/shard_map/ppermute | solution.py:22
  66.6 27.3 %collective-permute-start.5 = (bf16[256,192]{1,0:T(8,128)(2,1)S(1)}, bf16[256,192]{1,0:T(8,128)(2,1)S(1)}, u32[]{:S(2)}, u32[]{:S(2)}) collective-permute-start(bf16[256,192]{1,0:T(8,128)(2,1)S(1)} %copy.200), channel_id=1, source_target_pairs={{0,1},{1,0},{2,3},{3,2},{4,5},{5,4},{6,7},{7,6},{8,9},{9,8},{10,11... | collective-permute-start | bytes 294920 | tf_op jit(solution)/shard_map/ppermute | solution.py:18
  97.1 10.6 %collective-permute-start.7 = (bf16[256,768]{1,0:T(8,128)(2,1)S(1)}, bf16[256,768]{1,0:T(8,128)(2,1)S(1)}, u32[]{:S(2)}, u32[]{:S(2)}) collective-permute-start(bf16[256,768]{1,0:T(8,128)(2,1)S(1)} %add_convert_fusion.2), channel_id=1, source_target_pairs={{0,2},{2,0},{1,3},{3,1},{4,6},{6,4},{5,7},{7,5},{8,10},{10,8},{9,1... | collective-permute-start | bytes 1179656 | tf_op jit(solution)/shard_map/ppermute | solution.py:22
  98.4 12.2 %collective-permute-start.6 = (bf16[256,768]{1,0:T(8,128)(2,1)S(1)}, bf16[256,768]{1,0:T(8,128)(2,1)S(1)}, u32[]{:S(2)}, u32[]{:S(2)}) collective-permute-start(bf16[256,768]{1,0:T(8,128)(2,1)S(1)} %add_convert_fusion.2), channel_id=1, source_target_pairs={{0,1},{1,0},{2,3},{3,2},{4,5},{5,4},{6,7},{7,6},{8,9},{9,8},{10,11... | collective-permute-start | bytes 1179656 | tf_op jit(solution)/shard_map/ppermute | solution.py:18
  126.2 11.9 %collective-permute-start.11 = (bf16[256,768]{1,0:T(8,128)(2,1)S(1)}, bf16[256,768]{1,0:T(8,128)(2,1)S(1)}, u32[]{:S(2)}, u32[]{:S(2)}) collective-permute-start(bf16[256,768]{1,0:T(8,128)(2,1)S(1)} %fusion.53), channel_id=1, source_target_pairs={{0,2},{2,0},{1,3},{3,1},{4,6},{6,4},{5,7},{7,5},{8,10},{10,8},{9,1... | collective-permute-start | bytes 1179656 | tf_op jit(solution)/shard_map/ppermute | solution.py:22
  140.5 11.0 %collective-permute-start.13 = (bf16[256,768]{1,0:T(8,128)(2,1)S(1)}, bf16[256,768]{1,0:T(8,128)(2,1)S(1)}, u32[]{:S(2)}, u32[]{:S(2)}) collective-permute-start(bf16[256,768]{1,0:T(8,128)(2,1)S(1)} %convert_element_type.174), channel_id=1, source_target_pairs={{0,2},{2,0},{1,3},{3,1},{4,6},{6,4},{5,7},{7,5},{8,10},{10,8},{9,1... | collective-permute-start | bytes 1179656 | tf_op jit(solution)/shard_map/ppermute | solution.py:22
  141.8 11.9 %collective-permute-start.12 = (bf16[256,768]{1,0:T(8,128)(2,1)S(1)}, bf16[256,768]{1,0:T(8,128)(2,1)S(1)}, u32[]{:S(2)}, u32[]{:S(2)}) collective-permute-start(bf16[256,768]{1,0:T(8,128)(2,1)S(1)} %convert_element_type.174), channel_id=1, source_target_pairs={{0,1},{1,0},{2,3},{3,2},{4,5},{5,4},{6,7},{7,6},{8,9},{9,8},{10,11... | collective-permute-start | bytes 1179656 | tf_op jit(solution)/shard_map/ppermute | solution.py:18
  171.2 11.9 %collective-permute-start.17 = (bf16[256,768]{1,0:T(8,128)(2,1)S(1)}, bf16[256,768]{1,0:T(8,128)(2,1)S(1)}, u32[]{:S(2)}, u32[]{:S(2)}) collective-permute-start(bf16[256,768]{1,0:T(8,128)(2,1)S(1)} %fusion.50), channel_id=1, source_target_pairs={{0,2},{2,0},{1,3},{3,1},{4,6},{6,4},{5,7},{7,5},{8,10},{10,8},{9,1... | collective-permute-start | bytes 1179656 | tf_op jit(solution)/shard_map/ppermute | solution.py:22
  191.2 8.3 %collective-permute-start.20 = (bf16[256,192]{1,0:T(8,128)(2,1)S(1)}, bf16[256,192]{1,0:T(8,128)(2,1)S(1)}, u32[]{:S(2)}, u32[]{:S(2)}) collective-permute-start(bf16[256,192]{1,0:T(8,128)(2,1)S(1)} %get-tuple-element.67), channel_id=1, source_target_pairs={{0,3},{1,2},{2,1},{3,0},{4,7},{5,6},{6,5},{7,4},{8,11},{9,10},{10,... | collective-permute-start | bytes 294920 | tf_op jit(solution)/shard_map/ppermute | solution.py:26
  196.1 49.4 %collective-permute-start.27 = (bf16[768,192]{0,1:T(8,128)(2,1)}, bf16[768,192]{0,1:T(8,128)(2,1)}, u32[]{:S(2)}, u32[]{:S(2)}) collective-permute-start(bf16[768,192]{0,1:T(8,128)(2,1)} %convolution_convert_fusion.5), channel_id=1, source_target_pairs={{0,1},{1,0},{2,3},{3,2},{4,5},{5,4},{6,7},{7,6},{8,9},{9,8},{10,11... | collective-permute-start | bytes 884744 | tf_op jit(solution)/shard_map/ppermute | solution.py:18
  196.2 40.5 %collective-permute-start.28 = (bf16[768,192]{0,1:T(8,128)(2,1)}, bf16[768,192]{0,1:T(8,128)(2,1)}, u32[]{:S(2)}, u32[]{:S(2)}) collective-permute-start(bf16[768,192]{0,1:T(8,128)(2,1)} %convolution_convert_fusion.4), channel_id=1, source_target_pairs={{0,1},{1,0},{2,3},{3,2},{4,5},{5,4},{6,7},{7,6},{8,9},{9,8},{10,11... | collective-permute-start | bytes 884744 | tf_op jit(solution)/shard_map/ppermute | solution.py:18
  229.2 32.0 %all-to-all-start.2 = ((bf16[32,24,640]{2,1,0:T(8,128)(2,1)}), bf16[32,24,640]{2,1,0:T(8,128)(2,1)}, u32[]{:S(2)}, u32[]{:S(2)}) async-start(bf16[32,24,640]{2,1,0:T(8,128)(2,1)} %pad_maximum_fusion.5), calls=%async_computation.2 | async-start | bytes 1966080 | tf_op jit(solution)/shard_map/all_to_all | solution.py:76
  238.2 17.1 %collective-permute-start.29 = (bf16[768,192]{0,1:T(8,128)(2,1)S(1)}, bf16[768,192]{0,1:T(8,128)(2,1)S(1)}, u32[]{:S(2)}, u32[]{:S(2)}) collective-permute-start(bf16[768,192]{0,1:T(8,128)(2,1)S(1)} %fusion.22), channel_id=1, source_target_pairs={{0,2},{2,0},{1,3},{3,1},{4,6},{6,4},{5,7},{7,5},{8,10},{10,8},{9,1... | collective-permute-start | bytes 884744 | tf_op jit(solution)/shard_map/ppermute | solution.py:22
  242.2 32.6 %collective-permute-start.21 = (bf16[256,768]{1,0:T(8,128)(2,1)}, bf16[256,768]{1,0:T(8,128)(2,1)}, u32[]{:S(2)}, u32[]{:S(2)}) collective-permute-start(bf16[256,768]{1,0:T(8,128)(2,1)} %get-tuple-element.46), channel_id=1, source_target_pairs={{0,1},{1,0},{2,3},{3,2},{4,5},{5,4},{6,7},{7,6},{8,9},{9,8},{10,11... | collective-permute-start | bytes 1179656 | tf_op jit(solution)/shard_map/ppermute | solution.py:18
  244.7 30.1 %collective-permute-start.23 = (bf16[256,768]{1,0:T(8,128)(2,1)}, bf16[256,768]{1,0:T(8,128)(2,1)}, u32[]{:S(2)}, u32[]{:S(2)}) collective-permute-start(bf16[256,768]{1,0:T(8,128)(2,1)} %fusion.46), channel_id=1, source_target_pairs={{0,2},{2,0},{1,3},{3,1},{4,6},{6,4},{5,7},{7,5},{8,10},{10,8},{9,1... | collective-permute-start | bytes 1179656 | tf_op jit(solution)/shard_map/ppermute | solution.py:22
  261.2 46.9 %all-to-all-start.3 = ((bf16[32,24,1728]{2,1,0:T(8,128)(2,1)}), bf16[32,24,1728]{2,1,0:T(8,128)(2,1)S(1)}, u32[]{:S(2)}, u32[]{:S(2)}) async-start(bf16[32,24,1728]{2,1,0:T(8,128)(2,1)} %bitcast.35), calls=%async_computation.3 | async-start | bytes 5505024 | tf_op jit(solution)/shard_map/all_to_all | solution.py:76
  271.6 29.4 %collective-permute-start.25 = (f32[24,640]{1,0:T(8,128)S(1)}, f32[24,640]{1,0:T(8,128)S(1)}, u32[]{:S(2)}, u32[]{:S(2)}) collective-permute-start(f32[24,640]{1,0:T(8,128)S(1)} %convert_reduce_fusion.2), channel_id=1, source_target_pairs={{0,2},{2,0},{1,3},{3,1},{4,6},{6,4},{5,7},{7,5},{8,10},{10,8},{9,1... | collective-permute-start | bytes 184328 | tf_op jit(solution)/shard_map/ppermute | solution.py:22
  273.4 30.7 %collective-permute-start.24 = (f32[24,640]{1,0:T(8,128)S(1)}, f32[24,640]{1,0:T(8,128)S(1)}, u32[]{:S(2)}, u32[]{:S(2)}) collective-permute-start(f32[24,640]{1,0:T(8,128)S(1)} %convert_reduce_fusion.2), channel_id=1, source_target_pairs={{0,3},{1,2},{2,1},{3,0},{4,7},{5,6},{6,5},{7,4},{8,11},{9,10},{10,... | collective-permute-start | bytes 184328 | tf_op jit(solution)/shard_map/ppermute | solution.py:26
  309.9 10.1 %collective-permute-start.30 = (f32[24,1728]{1,0:T(8,128)S(1)}, f32[24,1728]{1,0:T(8,128)S(1)}, u32[]{:S(2)}, u32[]{:S(2)}) collective-permute-start(f32[24,1728]{1,0:T(8,128)S(1)} %convert_reduce_fusion), channel_id=1, source_target_pairs={{0,3},{1,2},{2,1},{3,0},{4,7},{5,6},{6,5},{7,4},{8,11},{9,10},{10,... | collective-permute-start | bytes 497672 | tf_op jit(solution)/shard_map/ppermute | solution.py:26
  (72 other events, 705.8 us)

commit v2 on v1

--- a/solution.py
+++ b/solution.py
@@ -6,9 +6,9 @@
 
 H = 12
 HD = 64
-FSDP = "fsdp"
+FSDP = ("plane", "pair")
 SP = ("sp_0", "sp_1")
-FSDP_SP = ("fsdp", "sp_0", "sp_1")
+FSDP_SP = ("plane", "pair", "sp_0", "sp_1")
 EPS = 1e-05
 BF = jnp.bfloat16
 F32 = jnp.float32
@@ -26,24 +26,27 @@
     return lax.ppermute(value, SP, [(0, 3), (1, 2), (2, 1), (3, 0)])
 
 
-def gather_relative(value):
-    across = swap_chip(value)
-    return [value, swap_core(value), across, swap_core(across)]
+def swap_pair(value):
+    return lax.ppermute(value, "pair", [(0, 1), (1, 0)])
 
 
 def gather_direct(value):
     return [value, swap_core(value), swap_chip(value), swap_both(value)]
 
 
-def exchange_direct(parts):
-    return [parts[0], swap_core(parts[1]), swap_chip(parts[2]), swap_both(parts[3])]
-
-
-def reduce_relative(parts):
-    far = parts[2] + swap_core(parts[3].astype(BF)).astype(F32)
-    far = swap_chip(far.astype(BF)).astype(F32)
-    near = parts[0] + swap_core(parts[1].astype(BF)).astype(F32)
-    return near + far
+def gather_halves(value):
+    across = swap_chip(value)
+    near = jnp.concatenate([value, swap_core(value)], axis=0)
+    return near, jnp.concatenate([across, swap_core(across)], axis=0)
+
+
+def send_half(half):
+    rows = half.shape[0] // 2
+    return half[:rows] + swap_core(half[rows:].astype(BF)).astype(F32)
+
+
+def reduce_far(far):
+    return swap_chip(send_half(far).astype(BF)).astype(F32)
 
 
 def reorder(parts):
@@ -70,11 +73,23 @@
     return filled.reshape(-1, value.shape[-1])
 
 
-def collect(value):
-    count = lax.axis_size(FSDP)
-    blocks = value.reshape(count, value.shape[0] // count, value.shape[1])
-    blocks = lax.all_to_all(blocks, FSDP, split_axis=0, concat_axis=0, tiled=True)
-    return blocks.astype(F32).sum(axis=0)
+def spread_pairs(value):
+    other = swap_pair(value)
+    high = lax.axis_index("pair") == 1
+    both = jnp.stack([jnp.where(high, other, value), jnp.where(high, value, other)], axis=1)
+    copies = jnp.broadcast_to(both, (lax.axis_size("plane"), *both.shape))
+    filled = lax.all_to_all(copies, "plane", split_axis=0, concat_axis=0, tiled=True)
+    return [filled[:, k].reshape(-1, value.shape[-1]) for k in range(value.shape[0])]
+
+
+def collect(values):
+    count = lax.axis_size("plane")
+    blocks = jnp.stack([v.reshape(count, 2, -1, v.shape[-1]) for v in values], axis=2)
+    blocks = lax.all_to_all(blocks, "plane", split_axis=0, concat_axis=0, tiled=True)
+    summed = blocks.astype(F32).sum(axis=0)
+    high = lax.axis_index("pair") == 1
+    keep = jnp.where(high, summed[1], summed[0])
+    return keep + swap_pair(jnp.where(high, summed[0], summed[1]))
 
 
 def layer_norm(hidden, gain, shift):
@@ -165,6 +180,7 @@
     me = lax.axis_index("sp_0") * 2 + lax.axis_index("sp_1")
 
     mine_qkv = lax.dynamic_index_in_dim(w_qkv.reshape(depth, 3, members, span), me, 2, False)
+    mine_out = lax.dynamic_slice_in_dim(w_out, me * span, span, 1)
     mine_in = lax.dynamic_index_in_dim(w_in.reshape(depth, shards, members, piece), me, 2, False)
     mine_back = lax.dynamic_index_in_dim(w_back.reshape(members, piece, width), me, 0, False)
     mine_bias = lax.dynamic_index_in_dim(bias_in.reshape(members, piece), me, 0, False)
@@ -172,19 +188,17 @@
         [bias_q, bias_v, bias_o, gain_one, shift_one, bias_back, gain_two, shift_two, mine_bias],
         axis=1,
     )
-    vectors = jnp.pad(vectors, ((0, 0), (0, 64 - vectors.shape[1])))
-    first = spread(jnp.concatenate([mine_qkv.reshape(depth, 3 * span), vectors], axis=1))
-    second = spread(
-        jnp.concatenate([w_out, mine_in.reshape(depth, hidden), mine_back], axis=1)
-    )
+    vectors = jnp.pad(vectors, ((0, 0), (0, 128 - vectors.shape[1])))
+    first = spread(jnp.concatenate([mine_qkv.reshape(depth, 3 * span), mine_out, vectors], axis=1))
+    w_in_m, w_back_m = spread_pairs(jnp.stack([mine_in.reshape(depth, hidden), mine_back]))
     w_qkv_m = first[:, : 3 * span]
-    small = first[:, 3 * span :].astype(F32).T
+    w_out_m = first[:, 3 * span : 4 * span]
+    small = first[:, 4 * span :].astype(F32).T
     b_q, b_v, b_o, g_one, s_one, b_back, g_two, s_two, b_in = [small[k] for k in range(9)]
-    w_out_all = second[:, :width]
-    w_in_m = second[:, width : width + hidden]
-    w_back_m = second[:, width + hidden :]
-
-    x_all = jnp.concatenate(gather_relative(tokens), axis=0)
+    w_out_all = jnp.concatenate(reorder(gather_direct(w_out_m)), axis=1)
+
+    x_near, x_far = gather_halves(tokens)
+    x_all = jnp.concatenate([x_near, x_far], axis=0)
     own_q = lax.dynamic_slice_in_dim(b_q, me * span, span, 0)
     own_v = lax.dynamic_slice_in_dim(b_v, me * span, span, 0)
     bias_qkv = jnp.concatenate([own_q, jnp.zeros((span,), F32), own_v])
@@ -195,20 +209,26 @@
     place = jnp.arange(members, dtype=jnp.int32) ^ me
     position = (place[:, None] * rows + jnp.arange(rows, dtype=jnp.int32)).reshape(total)
     valid = position < lengths[0]
-    context, logsum = attend_heads(query, keys, values, valid, scale)
-
-    parts = context.reshape(members, rows, span)
-    ctx_rows = jnp.concatenate(
-        reorder(exchange_direct([parts[m] for m in range(members)])), axis=1
-    )
+    half = total // 2
+    context_far, logsum_far = attend_heads(query[half:], keys, values, valid, scale)
+    far = context_far.reshape(2, rows, span)
+    far = [swap_chip(far[0]), swap_both(far[1])]
+    context_near, logsum_near = attend_heads(query[:half], keys, values, valid, scale)
+    near = context_near.reshape(2, rows, span)
+    ctx_rows = jnp.concatenate(reorder([near[0], swap_core(near[1]), *far]), axis=1)
     h_one = tokens.astype(F32) + dot(ctx_rows, w_out_all) + b_o
     y_one, n_one, i_one = layer_norm(h_one, g_one, s_one)
     y_oneb = y_one.astype(BF)
-    y_all = jnp.concatenate(gather_relative(y_oneb), axis=0)
-    pre = dot(y_all, w_in_m) + b_in
-    act = gelu_exact(pre).astype(BF)
-    partial = dot(act, w_back_m).reshape(members, rows, width)
-    h_two = y_oneb.astype(F32) + b_back + reduce_relative(partial)
+
+    def forward(y):
+        pre = dot(y, w_in_m) + b_in
+        act = gelu_exact(pre).astype(BF)
+        return pre, act, dot(act, w_back_m)
+
+    y_near, y_far = gather_halves(y_oneb)
+    pre_near, act_near, partial_near = forward(y_near)
+    pre_far, act_far, partial_far = forward(y_far)
+    h_two = y_oneb.astype(F32) + b_back + send_half(partial_near) + reduce_far(partial_far)
     out, n_two, i_two = layer_norm(h_two, g_two, s_two)
 
     grad = cotangent.astype(F32)
@@ -216,15 +236,22 @@
     d_s2 = jnp.sum(grad, axis=0)
     dh_two = norm_back(grad, n_two, i_two, g_two)
     d_bb = jnp.sum(dh_two, axis=0)
-    dh_all = jnp.concatenate(gather_relative(dh_two.astype(BF)), axis=0)
-    d_act = contract_cols(dh_all, w_back_m)
-    d_pre = jax.vjp(gelu_exact, pre)[1](d_act)[0]
-    d_preb = d_pre.astype(BF)
-    back = contract_cols(d_preb, w_in_m).reshape(members, rows, width)
-    dy_one = dh_two + reduce_relative(back)
-    d_bi = jnp.sum(d_pre, axis=0)
-    d_wb = contract_rows(act, dh_all)
-    d_wi = contract_rows(y_all, d_preb)
+
+    def backward(dh, pre):
+        d_pre = jax.vjp(gelu_exact, pre)[1](contract_cols(dh, w_back_m))[0]
+        d_preb = d_pre.astype(BF)
+        return d_preb, jnp.sum(d_pre, axis=0), contract_cols(d_preb, w_in_m)
+
+    dh_near, dh_far = gather_halves(dh_two.astype(BF))
+    d_pre_near, d_bi_near, back_near = backward(dh_near, pre_near)
+    d_pre_far, d_bi_far, back_far = backward(dh_far, pre_far)
+    dy_one = dh_two + send_half(back_near) + reduce_far(back_far)
+    d_bi = d_bi_near + d_bi_far
+    d_wb = (contract_rows(act_near, dh_near) + contract_rows(act_far, dh_far)).astype(BF)
+    d_wi = (contract_rows(y_near, d_pre_near) + contract_rows(y_far, d_pre_far)).astype(BF)
+    d_wi, d_wb, dy_one = lax.optimization_barrier((d_wi, d_wb, dy_one))
+    early = collect([d_wi, d_wb])
+    early = reorder(gather_direct(early))
 
     d_g1 = jnp.sum(dy_one * n_one, axis=0)
     d_s1 = jnp.sum(dy_one, axis=0)
@@ -232,40 +259,44 @@
     d_bo = jnp.sum(dh_one, axis=0)
     dh_oneb = dh_one.astype(BF)
     d_ctx = contract_cols(dh_oneb, w_out_all).astype(BF)
-    pieces = exchange_direct(reorder([d_ctx[:, m * span : (m + 1) * span] for m in range(members)]))
+    pieces = reorder([d_ctx[:, m * span : (m + 1) * span] for m in range(members)])
+    pieces = [pieces[0], swap_core(pieces[1]), swap_chip(pieces[2]), swap_both(pieces[3])]
     grad_heads = jnp.concatenate(pieces, axis=0).reshape(total, local, HD)
 
     columns = reorder([dh_oneb[:, m * span : (m + 1) * span] for m in range(members)])
-    d_wo = reduce_relative([contract_rows(ctx_rows, column) for column in columns])
-    early = collect(jnp.concatenate([d_wo.astype(BF), d_wi.astype(BF), d_wb.astype(BF)], axis=1))
-    early = reorder(gather_direct(early))
-
+    d_wo = [contract_rows(ctx_rows, column) for column in columns]
+    d_wo_far = reduce_far(jnp.concatenate(d_wo[2:], axis=0))
+    d_wo = send_half(jnp.concatenate(d_wo[:2], axis=0)) + d_wo_far
+
+    context = jnp.concatenate([context_near, context_far], axis=0)
+    logsum = jnp.concatenate([logsum_near, logsum_far], axis=1)
     g_query, g_keys, g_values = attend_back(
         query, keys, values, context, logsum, grad_heads, valid, scale
     )
     d_packed = jnp.concatenate(
         [g.reshape(total, span) for g in (g_query, g_keys, g_values)], axis=1
     )
-    d_x = dh_one + reduce_relative(contract_cols(d_packed, w_qkv_m).reshape(members, rows, width))
+    d_x_far = reduce_far(contract_cols(d_packed[half:], w_qkv_m))
+    d_x = dh_one + send_half(contract_cols(d_packed[:half], w_qkv_m)) + d_x_far
     d_wq = contract_rows(x_all, d_packed)
     empty = jnp.zeros((width,), F32)
     own = jnp.sum(d_packed.astype(F32), axis=0)
     d_bq = lax.dynamic_update_slice_in_dim(empty, own[:span], me * span, 0)
     d_bv = lax.dynamic_update_slice_in_dim(empty, own[2 * span :], me * span, 0)
     sums = jnp.stack([d_bq, d_bv, d_bo, d_g1, d_s1, d_bb, d_g2, d_s2, d_bi], axis=1)
-    sums = jnp.pad(sums, ((0, 0), (0, 64 - sums.shape[1])))
-    late = collect(jnp.concatenate([d_wq, sums], axis=1).astype(BF))
+    sums = jnp.pad(sums, ((0, 0), (0, 128 - sums.shape[1])))
+    late = collect([jnp.concatenate([d_wq, d_wo, sums], axis=1).astype(BF)])[0]
     late = reorder(gather_direct(late))
 
     grad_qkv = (
         jnp.stack([part[:, : 3 * span].reshape(depth, 3, span) for part in late], axis=2)
     ).reshape(depth, 3 * width)
-    grad_out = jnp.concatenate([part[:, :span] for part in early], axis=1)
-    grad_in = jnp.stack(
-        [part[:, span : span + hidden].reshape(depth, shards, piece) for part in early], axis=2
-    ).reshape(depth, members * hidden)
-    grad_back = jnp.concatenate([part[:, span + hidden :] for part in early], axis=0)
-    tails = [part[:, 3 * span : 3 * span + 9].T for part in late]
+    grad_out = jnp.concatenate([part[:, 3 * span : 4 * span] for part in late], axis=1)
+    grad_in = jnp.stack([part[0].reshape(depth, shards, piece) for part in early], axis=2).reshape(
+        depth, members * hidden
+    )
+    grad_back = jnp.concatenate([part[1] for part in early], axis=0)
+    tails = [part[:, 4 * span : 4 * span + 9].T for part in late]
     summed = tails[0] + tails[1] + tails[2] + tails[3]
     grad_bias_in = jnp.concatenate([tail[8] for tail in tails])
     return (
@@ -288,8 +319,9 @@
 
 
 def solution(mesh):
-    split = Mesh(mesh.devices.reshape(mesh.shape["fsdp"], 2, 2), FSDP_SP)
-    rows, flat = P("fsdp", None), P("fsdp")
+    planes = mesh.shape["fsdp"] // 2
+    split = Mesh(mesh.devices.reshape(planes, 2, 2, 2), FSDP_SP)
+    rows, flat = P(FSDP, None), P(FSDP)
     both = P(FSDP_SP, None)
     in_specs = (both, flat, rows, rows, rows, rows, *(flat,) * 9, both)
     out_specs = (both, both, rows, rows, rows, rows, *(flat,) * 9)

time: 333 us -> 352 us (1.057)
  starting transfers between devices: 70.1 us -> 76.4 us
  matrix products: 69.7 us -> 74.8 us
    all_to_all x2 -> x3, waiting for transfers between devices: 0.01 us -> 48.8 us  [the longest x2 33.1 us: collect(): lax.all_to_all(blocks, 'plane', split_axis=0, concat_axis=0, tiled=True)]
    ppermute x4 -> x5, waiting for transfers between devices: 37.2 us -> 9.05 us  [swap_both(): return lax.ppermute(value, SP, [(0, 3), (1, 2), (2, 1), (3, 0)])]
    all_to_all x2 -> x1, waiting for transfers between devices: 8.82 us -> 0.01 us  [spread(): lax.all_to_all(copies, FSDP, split_axis=0, concat_axis=0, tiled=True)]
    dot_general x4 -> x7, matrix products: 15.9 us -> 7.43 us  [contract_cols(): lax.dot_general(left, right, (((1,), (1,)), ((), ())), preferred_element_...]
    ppermute x11 -> x12, waiting for transfers between devices: 66.5 us -> 58.2 us  [swap_chip(): return lax.ppermute(value, 'sp_0', [(0, 1), (1, 0)])]
    dot_general x0 -> x1, matrix products: none -> 6.41 us  [attend_back(): jnp.einsum('qhd,khd->hqk', query, keys, preferred_element_type=F32) * scale]
    another operation x8 -> x7, local copies, waits for them, and re-layouts: 5.41 us -> 0.1 us  [body(): jnp.stack([d_bq, d_bv, d_bo, d_g1, d_s1, d_bb, d_g2, d_s2, d_bi], axis=1)]
    unnamed x122 -> x88, local copies, waits for them, and re-layouts: 5.09 us -> 9.32 us
  transfers between devices with their start and end apart: 37 -> 43, of which waited for: 15 -> 17; matrix products, arithmetic and copies ran while one was open for 28% -> 33% of each run, Pallas kernels for 0% -> 0%
where the time goes in v2:
time: 352 us; the launch traced here: 346 us
  waiting for transfers between devices  119 us (34%)
  starting transfers between devices  76.4 us (22%)
  matrix products  74.8 us (21%)
  local copies, waits for them, and re-layouts  47.2 us (13%)
  other arithmetic  25.7 us (7%)
    ppermute x12, waiting for transfers between devices, swap_chip(): return lax.ppermute(value, 'sp_0', [(0, 1), (1, 0)])  58.2 us
    all_to_all x2, waiting for transfers between devices, collect(): lax.all_to_all(blocks, 'plane', split_axis=0, concat_axis=0, tiled=True)  33.1 us
    dot_general x6, matrix products, dot(): return jnp.dot(left, right, preferred_element_type=F32)  20.3 us
    ppermute x19, starting transfers between devices, swap_core(): return lax.ppermute(value, 'sp_1', [(0, 1), (1, 0)])  19.9 us
    ppermute x12, starting transfers between devices, swap_chip(): return lax.ppermute(value, 'sp_0', [(0, 1), (1, 0)])  19.3 us
    dot_general x9, matrix products, contract_rows(): lax.dot_general(left, right, (((0,), (0,)), ((), ())), preferred_element_...  16.7 us
    all_to_all x1, waiting for transfers between devices, spread_pairs(): lax.all_to_all(copies, 'plane', split_axis=0, concat_axis=0, tiled=True)  15.7 us
    all_to_all x1, starting transfers between devices, spread(): lax.all_to_all(copies, FSDP, split_axis=0, concat_axis=0, tiled=True)  9.93 us
  transfers between devices with their start and end apart: 43, of which 17 were waited for; matrix products, arithmetic and copies ran while one was open for 33% of the time, Pallas kernels for 0%

profile of v2, /device:TPU:1, one launch (start us, length us, event | category | flops | bytes accessed | tf_op | source)
XLA Modules:
  0.0 346.3 jit_solution(15856292533060984986)
XLA Ops:
  11.1 9.9 %all-to-all-start = ((bf16[32,24,896]{2,1,0:T(8,128)(2,1)}), bf16[32,24,896]{2,1,0:T(8,128)(2,1)S(1)}, u32[]{:S(2)}, u32[]{:S(2)}) async-start(bf16[32,24,896]{2,1,0:T(8,128)(2,1)} %broadcast_in_dim.32), calls=%async_computation | async-start | bytes 2752512 | tf_op jit(solution)/shard_map/all_to_all | solution.py:72
  30.0 17.1 %collective-permute-done.1 = bf16[256,768]{1,0:T(8,128)(2,1)} collective-permute-done((bf16[256,768]{1,0:T(8,128)(2,1)S(1)}, bf16[256,768]{1,0:T(8,128)(2,1)}, u32[]{:S(2)}, u32[]{:S(2)}) %collective-permute-start.1) | collective-permute-done | bytes 393248 | tf_op jit(solution)/shard_map/ppermute | solution.py:22
  65.5 2.8 fusion.7
  80.4 6.5 %all-to-all-start.1 = ((bf16[16,2,2,24,768]{4,3,2,1,0:T(8,128)(2,1)}), bf16[16,2,2,24,768]{4,3,2,1,0:T(8,128)(2,1)}, u32[]{:S(2)}, u32[]{:S(2)}) async-start(bf16[16,2,2,24,768]{4,3,2,1,0:T(8,128)(2,1)} %broadcast_in_dim.64), calls=%async_computation.1 | async-start | bytes 4718592 | tf_op jit(solution)/shard_map/all_to_all | solution.py:81
  94.7 9.2 %collective-permute-done.12 = bf16[256,768]{1,0:T(8,128)(2,1)} collective-permute-done((bf16[256,768]{1,0:T(8,128)(2,1)}, bf16[256,768]{1,0:T(8,128)(2,1)}, u32[]{:S(2)}, u32[]{:S(2)}) %collective-permute-start.12) | collective-permute-done | bytes 393248 | tf_op jit(solution)/shard_map/ppermute | solution.py:22
  107.6 15.7 %all-to-all-done.1 = bf16[16,2,2,24,768]{4,3,2,1,0:T(8,128)(2,1)} async-done(((bf16[16,2,2,24,768]{4,3,2,1,0:T(8,128)(2,1)}), bf16[16,2,2,24,768]{4,3,2,1,0:T(8,128)(2,1)}, u32[]{:S(2)}, u32[]{:S(2)}) %all-to-all-start.1) | async-done | bytes 2359328 | tf_op jit(solution)/shard_map/all_to_all | solution.py:81
  126.2 10.2 %multiply_convert_fusion.1 = (bf16[512,768]{1,0:T(8,128)(2,1)S(1)}, f32[512,768]{1,0:T(8,128)S(1)}, f32[512,768]{1,0:T(8,128)S(1)}) fusion(f32[768]{0:T(1024)S(1)} %get-tuple-element.30, bf16[512,768]{1,0:T(8,128)(2,1)S(1)} %constant_dynamic-update-slice_fusion.4, bf16[768,768]{1,0:T(8,128)(2,1)S(1)} %bitcast.164), kind=kOutput, calls=%fused_computation.31 | convolution fusion | flops 629932032 | bytes 5901312 | tf_op jit(solution)/shard_map/dot_general | solution.py:116
  138.7 5.1 %multiply_convert_fusion.2 = (bf16[512,768]{1,0:T(8,128)(2,1)S(1)}, f32[512,768]{1,0:T(8,128)S(1)}, f32[512,768]{1,0:T(8,128)S(1)}) fusion(f32[768]{0:T(1024)S(1)} %get-tuple-element.30, bf16[768,768]{1,0:T(8,128)(2,1)S(1)} %bitcast.165, bf16[256,768]{1,0:T(8,128)(2,1)} %collective-permute-done.9, bf16[256,768]{1,0:T(8,128)(2,1)} %add_convert_fusion.4), kind=kOutput, calls=%fused_computation.44 | convolution fusion | flops 631504896 | bytes 5901312 | tf_op jit(solution)/shard_map/dot_general | solution.py:116
  146.5 10.2 %collective-permute-done.15 = bf16[256,768]{1,0:T(8,128)(2,1)S(1)} collective-permute-done((bf16[256,768]{1,0:T(8,128)(2,1)S(1)}, bf16[256,768]{1,0:T(8,128)(2,1)S(1)}, u32[]{:S(2)}, u32[]{:S(2)}) %collective-permute-start.15) | collective-permute-done | bytes 393248 | tf_op jit(solution)/shard_map/ppermute | solution.py:22
  160.4 6.4 %fusion.112 = f32[3,1024,1024]{2,1,0:T(8,128)} fusion(bf16[1024,3,64]{0,2,1:T(8,128)(2,1)S(1)} %bitcast.155, bf16[1024,3,64]{0,2,1:T(8,128)(2,1)S(1)} %bitcast.151), kind=kOutput, calls=%fused_computation.302 | convolution fusion | flops 402653184 | bytes 13369344 | tf_op jit(solution)/shard_map/qhd,khd->hqk/dot_general | solution.py:139
  170.8 8.3 %collective-permute-done.17 = bf16[256,768]{1,0:T(8,128)(2,1)S(1)} collective-permute-done((bf16[256,768]{1,0:T(8,128)(2,1)S(1)}, bf16[256,768]{1,0:T(8,128)(2,1)S(1)}, u32[]{:S(2)}, u32[]{:S(2)}) %collective-permute-start.17) | collective-permute-done | bytes 393248 | tf_op jit(solution)/shard_map/ppermute | solution.py:22
  191.1 8.8 %collective-permute-done.21 = bf16[256,768]{1,0:T(8,128)(2,1)S(1)} collective-permute-done((bf16[256,768]{1,0:T(8,128)(2,1)S(1)}, bf16[256,768]{1,0:T(8,128)(2,1)S(1)}, u32[]{:S(2)}, u32[]{:S(2)}) %collective-permute-start.21) | collective-permute-done | bytes 393248 | tf_op jit(solution)/shard_map/ppermute | solution.py:22
  212.0 3.1 collective-permute-done.24
  217.3 7.4 %fusion.23 = bf16[3,64,1024]{2,1,0:T(8,128)(2,1)S(1)} fusion(bf16[1024,3,64]{0,2,1:T(8,128)(2,1)} %bitcast.161, f32[3,1024,1024]{2,1,0:T(8,128)} %fusion.112, f32[3,1024]{1,0:T(4,128)S(1)} %pad_maximum_fusion.19, pred[1024]{0:T(1024)(128)(4,1)S(1)} %lt.34), kind=kOutput, calls=%fused_computation.67 | convolution fusion | flops 415432704 | bytes 13382656 | tf_op jit(solution)/shard_map/hqk,qhd->khd/dot_general | solution.py:143
  224.7 7.0 %multiply_convert_fusion = bf16[3,1024,1024]{2,1,0:T(8,128)(2,1)S(1)} fusion(f32[3,1024,1024]{2,1,0:T(8,128)} %fusion.112, f32[3,1024]{1,0:T(4,128)S(1)} %bitcast.183, f32[3,1024]{1,0:T(4,128)S(1)} %pad_maximum_fusion.19, pred[1024]{0:T(1024)(128)(4,1)S(1)} %lt.34, bf16[1024,3,64]{0,2,1:T(8,128)(2,1)S(1)} %bitcast.162, bf16[1024,3,64]{0,2,1:T(8,128)(2,1)S(1)} %bitcast.177), kind=kOutput, calls=%fused_computation | convolution fusion | flops 421527552 | bytes 19686400 | tf_op jit(solution)/shard_map/qhd,khd->hqk/dot_general | solution.py:144
  239.6 3.4 convolution_convert_fusion
  251.9 2.6 maximum_bitcast_fusion
  254.5 4.4 %all-to-all-start.2 = ((bf16[16,2,1,24,896]{4,3,1,2,0:T(8,128)(2,1)}), bf16[16,2,1,24,896]{4,3,1,2,0:T(8,128)(2,1)}, u32[]{:S(2)}, u32[]{:S(2)}) async-start(bf16[16,2,1,24,896]{4,3,1,2,0:T(8,128)(2,1)} %maximum_bitcast_fusion), calls=%async_computation.2 | async-start | bytes 2752512 | tf_op jit(solution)/shard_map/all_to_all | solution.py:88
  267.2 11.5 %all-to-all-done.2 = bf16[16,2,1,24,896]{4,3,1,2,0:T(8,128)(2,1)} async-done(((bf16[16,2,1,24,896]{4,3,1,2,0:T(8,128)(2,1)}), bf16[16,2,1,24,896]{4,3,1,2,0:T(8,128)(2,1)}, u32[]{:S(2)}, u32[]{:S(2)}) %all-to-all-start.2) | async-done | bytes 1376288 | tf_op jit(solution)/shard_map/all_to_all | solution.py:88
  283.2 5.3 %all-to-all-start.3 = ((bf16[16,2,2,24,768]{4,3,1,2,0:T(8,128)(2,1)}), bf16[16,2,2,24,768]{4,3,1,2,0:T(8,128)(2,1)S(1)}, u32[]{:S(2)}, u32[]{:S(2)}) async-start(bf16[16,2,2,24,768]{4,3,1,2,0:T(8,128)(2,1)} %pad_maximum_fusion), calls=%async_computation.3 | async-start | bytes 4718592 | tf_op jit(solution)/shard_map/all_to_all | solution.py:88
  295.8 2.6 collective-permute-done.32
  299.8 21.6 %all-to-all-done.3 = bf16[16,2,2,24,768]{4,3,1,2,0:T(8,128)(2,1)S(1)} async-done(((bf16[16,2,2,24,768]{4,3,1,2,0:T(8,128)(2,1)}), bf16[16,2,2,24,768]{4,3,1,2,0:T(8,128)(2,1)S(1)}, u32[]{:S(2)}, u32[]{:S(2)}) %all-to-all-start.3) | async-done | bytes 2359328 | tf_op jit(solution)/shard_map/all_to_all | solution.py:88
  325.8 3.9 %collective-permute-start.38 = (f32[2,24,768]{2,1,0:T(8,128)S(1)}, f32[2,24,768]{2,1,0:T(8,128)S(1)}, u32[]{:S(2)}, u32[]{:S(2)}) collective-permute-start(f32[2,24,768]{2,1,0:T(8,128)S(1)} %fusion.69), channel_id=1, source_target_pairs={{0,1},{1,0},{2,3},{3,2},{4,5},{5,4},{6,7},{7,6},{8,9},{9,8},{10,11... | collective-permute-start | bytes 442376 | tf_op jit(solution)/shard_map/ppermute | solution.py:18
  336.6 3.4 collective-permute-done.36
  (336 shorter events, 156.9 us)
Async XLA Ops:
  11.1 42.3 %all-to-all-start = ((bf16[32,24,896]{2,1,0:T(8,128)(2,1)}), bf16[32,24,896]{2,1,0:T(8,128)(2,1)S(1)}, u32[]{:S(2)}, u32[]{:S(2)}) async-start(bf16[32,24,896]{2,1,0:T(8,128)(2,1)} %broadcast_in_dim.32), calls=%async_computation | async-start | bytes 2752512 | tf_op jit(solution)/shard_map/all_to_all | solution.py:72
  21.1 29.0 %collective-permute-start = (bf16[256,768]{1,0:T(8,128)(2,1)S(1)}, bf16[256,768]{1,0:T(8,128)(2,1)S(1)}, u32[]{:S(2)}, u32[]{:S(2)}) collective-permute-start(bf16[256,768]{1,0:T(8,128)(2,1)S(1)} %copy-done.17), channel_id=1, source_target_pairs={{0,1},{1,0},{2,3},{3,2},{4,5},{5,4},{6,7},{7,6},{8,9},{9,8},{10,11... | collective-permute-start | bytes 1179656 | tf_op jit(solution)/shard_map/ppermute | solution.py:18
  22.1 25.0 %collective-permute-start.1 = (bf16[256,768]{1,0:T(8,128)(2,1)S(1)}, bf16[256,768]{1,0:T(8,128)(2,1)}, u32[]{:S(2)}, u32[]{:S(2)}) collective-permute-start(bf16[256,768]{1,0:T(8,128)(2,1)S(1)} %copy-done.17), channel_id=1, source_target_pairs={{0,2},{2,0},{1,3},{3,1},{4,6},{6,4},{5,7},{7,5},{8,10},{10,8},{9,1... | collective-permute-start | bytes 1179656 | tf_op jit(solution)/shard_map/ppermute | solution.py:22
  27.4 22.0 %collective-permute-start.10 = (bf16[2,24,768]{2,1,0:T(8,128)(2,1)S(1)}, bf16[2,24,768]{2,1,0:T(8,128)(2,1)S(1)}, u32[]{:S(2)}, u32[]{:S(2)}) collective-permute-start(bf16[2,24,768]{2,1,0:T(8,128)(2,1)S(1)} %pad_maximum_fusion.17), channel_id=1, source_target_pairs={{0,4},{4,0},{1,5},{5,1},{2,6},{6,2},{3,7},{7,3},{8,12},{12,8},{9,1... | collective-permute-start | bytes 221192 | tf_op jit(solution)/shard_map/ppermute | solution.py:30
  54.4 33.6 %collective-permute-start.8 = (bf16[768,192]{1,0:T(8,128)(2,1)}, bf16[768,192]{1,0:T(8,128)(2,1)}, u32[]{:S(2)}, u32[]{:S(2)}) collective-permute-start(bf16[768,192]{1,0:T(8,128)(2,1)} %slice.370), channel_id=1, source_target_pairs={{0,1},{1,0},{2,3},{3,2},{4,5},{5,4},{6,7},{7,6},{8,9},{9,8},{10,11... | collective-permute-start | bytes 884744 | tf_op jit(solution)/shard_map/ppermute | solution.py:18
  54.5 33.6 %collective-permute-start.7 = (bf16[768,192]{1,0:T(8,128)(2,1)}, bf16[768,192]{1,0:T(8,128)(2,1)}, u32[]{:S(2)}, u32[]{:S(2)}) collective-permute-start(bf16[768,192]{1,0:T(8,128)(2,1)} %slice.370), channel_id=1, source_target_pairs={{0,2},{2,0},{1,3},{3,1},{4,6},{6,4},{5,7},{7,5},{8,10},{10,8},{9,1... | collective-permute-start | bytes 884744 | tf_op jit(solution)/shard_map/ppermute | solution.py:22
  56.6 31.5 %collective-permute-start.6 = (bf16[768,192]{1,0:T(8,128)(2,1)}, bf16[768,192]{1,0:T(8,128)(2,1)}, u32[]{:S(2)}, u32[]{:S(2)}) collective-permute-start(bf16[768,192]{1,0:T(8,128)(2,1)} %slice.370), channel_id=1, source_target_pairs={{0,3},{1,2},{2,1},{3,0},{4,7},{5,6},{6,5},{7,4},{8,11},{9,10},{10,... | collective-permute-start | bytes 884744 | tf_op jit(solution)/shard_map/ppermute | solution.py:26
  74.5 12.6 %collective-permute-start.3 = (bf16[256,192]{1,0:T(8,128)(2,1)}, bf16[256,192]{1,0:T(8,128)(2,1)S(1)}, u32[]{:S(2)}, u32[]{:S(2)}) collective-permute-start(bf16[256,192]{1,0:T(8,128)(2,1)} %copy.94), channel_id=1, source_target_pairs={{0,3},{1,2},{2,1},{3,0},{4,7},{5,6},{6,5},{7,4},{8,11},{9,10},{10,... | collective-permute-start | bytes 294920 | tf_op jit(solution)/shard_map/ppermute | solution.py:26
  76.5 10.5 %collective-permute-start.4 = (bf16[256,192]{1,0:T(8,128)(2,1)}, bf16[256,192]{1,0:T(8,128)(2,1)}, u32[]{:S(2)}, u32[]{:S(2)}) collective-permute-start(bf16[256,192]{1,0:T(8,128)(2,1)} %copy.95), channel_id=1, source_target_pairs={{0,2},{2,0},{1,3},{3,1},{4,6},{6,4},{5,7},{7,5},{8,10},{10,8},{9,1... | collective-permute-start | bytes 294920 | tf_op jit(solution)/shard_map/ppermute | solution.py:22
  80.4 42.9 %all-to-all-start.1 = ((bf16[16,2,2,24,768]{4,3,2,1,0:T(8,128)(2,1)}), bf16[16,2,2,24,768]{4,3,2,1,0:T(8,128)(2,1)}, u32[]{:S(2)}, u32[]{:S(2)}) async-start(bf16[16,2,2,24,768]{4,3,2,1,0:T(8,128)(2,1)} %broadcast_in_dim.64), calls=%async_computation.1 | async-start | bytes 4718592 | tf_op jit(solution)/shard_map/all_to_all | solution.py:81
  92.1 11.9 %collective-permute-start.12 = (bf16[256,768]{1,0:T(8,128)(2,1)}, bf16[256,768]{1,0:T(8,128)(2,1)}, u32[]{:S(2)}, u32[]{:S(2)}) collective-permute-start(bf16[256,768]{1,0:T(8,128)(2,1)} %add_convert_fusion.4), channel_id=1, source_target_pairs={{0,2},{2,0},{1,3},{3,1},{4,6},{6,4},{5,7},{7,5},{8,10},{10,8},{9,1... | collective-permute-start | bytes 1179656 | tf_op jit(solution)/shard_map/ppermute | solution.py:22
  93.7 45.0 %collective-permute-start.9 = (bf16[256,768]{1,0:T(8,128)(2,1)}, bf16[256,768]{1,0:T(8,128)(2,1)}, u32[]{:S(2)}, u32[]{:S(2)}) collective-permute-start(bf16[256,768]{1,0:T(8,128)(2,1)} %add_convert_fusion.4), channel_id=1, source_target_pairs={{0,1},{1,0},{2,3},{3,2},{4,5},{5,4},{6,7},{7,6},{8,9},{9,8},{10,11... | collective-permute-start | bytes 1179656 | tf_op jit(solution)/shard_map/ppermute | solution.py:18
  104.0 21.2 %collective-permute-start.13 = (bf16[256,768]{1,0:T(8,128)(2,1)}, bf16[256,768]{1,0:T(8,128)(2,1)}, u32[]{:S(2)}, u32[]{:S(2)}) collective-permute-start(bf16[256,768]{1,0:T(8,128)(2,1)} %collective-permute-done.12), channel_id=1, source_target_pairs={{0,1},{1,0},{2,3},{3,2},{4,5},{5,4},{6,7},{7,6},{8,9},{9,8},{10,11... | collective-permute-start | bytes 1179656 | tf_op jit(solution)/shard_map/ppermute | solution.py:18
  144.9 11.8 %collective-permute-start.15 = (bf16[256,768]{1,0:T(8,128)(2,1)S(1)}, bf16[256,768]{1,0:T(8,128)(2,1)S(1)}, u32[]{:S(2)}, u32[]{:S(2)}) collective-permute-start(bf16[256,768]{1,0:T(8,128)(2,1)S(1)} %fusion.49), channel_id=1, source_target_pairs={{0,2},{2,0},{1,3},{3,1},{4,6},{6,4},{5,7},{7,5},{8,10},{10,8},{9,1... | collective-permute-start | bytes 1179656 | tf_op jit(solution)/shard_map/ppermute | solution.py:22
  166.8 12.3 %collective-permute-start.17 = (bf16[256,768]{1,0:T(8,128)(2,1)S(1)}, bf16[256,768]{1,0:T(8,128)(2,1)S(1)}, u32[]{:S(2)}, u32[]{:S(2)}) collective-permute-start(bf16[256,768]{1,0:T(8,128)(2,1)S(1)} %convert_element_type.196), channel_id=1, source_target_pairs={{0,2},{2,0},{1,3},{3,1},{4,6},{6,4},{5,7},{7,5},{8,10},{10,8},{9,1... | collective-permute-start | bytes 1179656 | tf_op jit(solution)/shard_map/ppermute | solution.py:22
  170.4 20.8 %collective-permute-start.19 = (bf16[256,768]{1,0:T(8,128)(2,1)S(1)}, bf16[256,768]{1,0:T(8,128)(2,1)S(1)}, u32[]{:S(2)}, u32[]{:S(2)}) collective-permute-start(bf16[256,768]{1,0:T(8,128)(2,1)S(1)} %slice.628), channel_id=1, source_target_pairs={{0,1},{1,0},{2,3},{3,2},{4,5},{5,4},{6,7},{7,6},{8,9},{9,8},{10,11... | collective-permute-start | bytes 1179656 | tf_op jit(solution)/shard_map/ppermute | solution.py:18
  187.8 12.1 %collective-permute-start.21 = (bf16[256,768]{1,0:T(8,128)(2,1)S(1)}, bf16[256,768]{1,0:T(8,128)(2,1)S(1)}, u32[]{:S(2)}, u32[]{:S(2)}) collective-permute-start(bf16[256,768]{1,0:T(8,128)(2,1)S(1)} %fusion.46), channel_id=1, source_target_pairs={{0,2},{2,0},{1,3},{3,1},{4,6},{6,4},{5,7},{7,5},{8,10},{10,8},{9,1... | collective-permute-start | bytes 1179656 | tf_op jit(solution)/shard_map/ppermute | solution.py:22
  209.9 36.2 %collective-permute-start.28 = (bf16[768,192]{0,1:T(8,128)(2,1)}, bf16[768,192]{0,1:T(8,128)(2,1)}, u32[]{:S(2)}, u32[]{:S(2)}) collective-permute-start(bf16[768,192]{0,1:T(8,128)(2,1)} %convolution_convert_fusion.3), channel_id=1, source_target_pairs={{0,1},{1,0},{2,3},{3,2},{4,5},{5,4},{6,7},{7,6},{8,9},{9,8},{10,11... | collective-permute-start | bytes 884744 | tf_op jit(solution)/shard_map/ppermute | solution.py:18
  210.1 25.1 %collective-permute-start.29 = (bf16[768,192]{0,1:T(8,128)(2,1)}, bf16[768,192]{0,1:T(8,128)(2,1)}, u32[]{:S(2)}, u32[]{:S(2)}) collective-permute-start(bf16[768,192]{0,1:T(8,128)(2,1)} %convolution_convert_fusion.2), channel_id=1, source_target_pairs={{0,1},{1,0},{2,3},{3,2},{4,5},{5,4},{6,7},{7,6},{8,9},{9,8},{10,11... | collective-permute-start | bytes 884744 | tf_op jit(solution)/shard_map/ppermute | solution.py:18
  238.2 10.3 %collective-permute-start.30 = (bf16[768,192]{0,1:T(8,128)(2,1)}, bf16[768,192]{0,1:T(8,128)(2,1)}, u32[]{:S(2)}, u32[]{:S(2)}) collective-permute-start(bf16[768,192]{0,1:T(8,128)(2,1)} %fusion.30), channel_id=1, source_target_pairs={{0,2},{2,0},{1,3},{3,1},{4,6},{6,4},{5,7},{7,5},{8,10},{10,8},{9,1... | collective-permute-start | bytes 884744 | tf_op jit(solution)/shard_map/ppermute | solution.py:22
  254.5 24.3 %all-to-all-start.2 = ((bf16[16,2,1,24,896]{4,3,1,2,0:T(8,128)(2,1)}), bf16[16,2,1,24,896]{4,3,1,2,0:T(8,128)(2,1)}, u32[]{:S(2)}, u32[]{:S(2)}) async-start(bf16[16,2,1,24,896]{4,3,1,2,0:T(8,128)(2,1)} %maximum_bitcast_fusion), calls=%async_computation.2 | async-start | bytes 2752512 | tf_op jit(solution)/shard_map/all_to_all | solution.py:88
  265.0 28.5 %collective-permute-start.25 = (bf16[256,768]{1,0:T(8,128)(2,1)}, bf16[256,768]{1,0:T(8,128)(2,1)}, u32[]{:S(2)}, u32[]{:S(2)}) collective-permute-start(bf16[256,768]{1,0:T(8,128)(2,1)} %slice.626), channel_id=1, source_target_pairs={{0,1},{1,0},{2,3},{3,2},{4,5},{5,4},{6,7},{7,6},{8,9},{9,8},{10,11... | collective-permute-start | bytes 1179656 | tf_op jit(solution)/shard_map/ppermute | solution.py:18
  265.9 27.6 %collective-permute-start.27 = (bf16[256,768]{1,0:T(8,128)(2,1)}, bf16[256,768]{1,0:T(8,128)(2,1)}, u32[]{:S(2)}, u32[]{:S(2)}) collective-permute-start(bf16[256,768]{1,0:T(8,128)(2,1)} %fusion.42), channel_id=1, source_target_pairs={{0,2},{2,0},{1,3},{3,1},{4,6},{6,4},{5,7},{7,5},{8,10},{10,8},{9,1... | collective-permute-start | bytes 1179656 | tf_op jit(solution)/shard_map/ppermute | solution.py:22
  283.2 38.2 %all-to-all-start.3 = ((bf16[16,2,2,24,768]{4,3,1,2,0:T(8,128)(2,1)}), bf16[16,2,2,24,768]{4,3,1,2,0:T(8,128)(2,1)S(1)}, u32[]{:S(2)}, u32[]{:S(2)}) async-start(bf16[16,2,2,24,768]{4,3,1,2,0:T(8,128)(2,1)} %pad_maximum_fusion), calls=%async_computation.3 | async-start | bytes 4718592 | tf_op jit(solution)/shard_map/all_to_all | solution.py:88
  (60 other events, 395.7 us)
